TPU v7x, 512 devices: a whole 4x8x8 slice. The times are simulated.
512 devices in a mesh: row: 16 (over z, y_lo), col: 32 (over x, y_hi, core).
Axes of the slice: x: 4, y: 8 (y_hi: 4, y_lo: 2; y = y_hi * 2 + y_lo), z: 8, core: 2. Of those that a mesh axis runs over, the one named last changes fastest.
Arguments:
- features: bfloat16 [65536, 128], P(('col', 'row')), may hold values from -6 to 6
- grad_out: bfloat16 [65536, 128], P(('row', 'col')), may hold values from -6 to 6
- weight: bfloat16 [128, 128], replicated, may hold values from -0.5 to 0.5
- block_ids: int32 [16, 32, 152], P('row', 'col'), may hold values from 0 to 511, as said below
- block_vals: bfloat16 [16, 32, 152, 128, 128], P('row', 'col'), may hold values from -0.0390625 to 0.0390625
- block_count: int32 [16, 32], P('row', 'col'), may hold values from 1 to 152
- node_perm: int32 [512, 128], P(('col', 'row')), may hold values from 0 to 127, each once within a row
Outputs:
- feature_grad: bfloat16 [65536, 128], P(('col', 'row'))
- weight_grad: float32 [128, 128], replicated
Inputs may be any that keep to these rules, and one draw needn't show every extreme that they name: `block_ids`: in each tile the 152 entries are distinct block positions p * 16 + q; slots at or beyond block_count are empty and must be ignored. `node_perm`: each row is a permutation of 0 to 127.
All inputs are finite; a program needn't handle non-finite values.
Results may differ from a plain program's by a relative error of at most 0.0059.
Values may be sent and summed in bfloat16 or wider, within the bound.
A program may use at most 128 MiB of HBM per device.

v0:
```python
import math

import jax
import jax.numpy as jnp
from jax import lax
from jax.sharding import PartitionSpec as P

BLOCK = 128


def grad_step(agg_low, grad_rows, weight):
    pre = jnp.dot(agg_low, weight, preferred_element_type=jnp.float32)
    sigma = jax.nn.sigmoid(pre)
    grad_pre = (grad_rows.astype(jnp.float32) * sigma * (1.0 + pre * (1.0 - sigma))).astype(
        jnp.bfloat16
    )
    grad_agg = lax.dot_general(
        grad_pre, weight, (((1,), (1,)), ((), ())), preferred_element_type=jnp.float32
    )
    return (grad_pre, grad_agg.astype(jnp.bfloat16))


def block_sums(product, targets, live, segments):
    routed = jnp.where(live, targets, segments)
    summed = jax.ops.segment_sum(product, routed, num_segments=segments + 1)
    return summed[:segments]


def shards(features, grad_out, weight, block_ids, block_vals, block_count, node_perm):
    nodes_dev = grad_out.shape[0]
    hidden = weight.shape[0]
    tile_ids = block_ids[0, 0]
    values = block_vals[0, 0]
    count_live = block_count[0, 0]
    slots_tile = tile_ids.shape[0]
    row_count = nodes_dev * lax.axis_size("col") // BLOCK
    col_count = nodes_dev * lax.axis_size("row") // BLOCK
    total_nodes = nodes_dev * lax.axis_size("row") * lax.axis_size("col")
    live = jnp.arange(slots_tile, dtype=jnp.int32) < count_live
    block_row = tile_ids // col_count
    block_col = tile_ids % col_count
    column_source = lax.all_gather(features, "row", axis=0, tiled=True)
    picked = column_source.reshape(col_count, BLOCK, hidden)[block_col]
    product = jnp.einsum("kij,kjf->kif", values, picked, preferred_element_type=jnp.float32)
    partial_value = block_sums(product, block_row, live, row_count).reshape(
        row_count * BLOCK, hidden
    )
    aggregate = lax.psum_scatter(partial_value, "col", scatter_dimension=0, tiled=True)
    agg_low = aggregate.astype(jnp.bfloat16)
    grad_pre, grad_share = grad_step(agg_low, grad_out, weight)
    weight_part = jnp.dot(agg_low.T, grad_pre, preferred_element_type=jnp.float32)
    grad_rows = lax.all_gather(grad_share, "col", axis=0, tiled=True)
    weight_grad = lax.psum(weight_part, ("row", "col")) * (1.0 / math.sqrt(total_nodes))
    picked_back = grad_rows.reshape(row_count, BLOCK, hidden)[block_row]
    product_back = jnp.einsum(
        "kij,kif->kjf", values, picked_back, preferred_element_type=jnp.float32
    )
    partial_back = block_sums(product_back, block_col, live, col_count).reshape(
        col_count * BLOCK, hidden
    )
    grad_share_cols = lax.psum_scatter(partial_back, "row", scatter_dimension=0, tiled=True)
    rounded = grad_share_cols.astype(jnp.bfloat16)
    feature_grad = rounded[node_perm[0]]
    return (feature_grad, weight_grad)


def solution(mesh):
    in_specs = (
        P(("col", "row"), None),
        P(("row", "col"), None),
        P(),
        P("row", "col", None),
        P("row", "col", None, None, None),
        P("row", "col"),
        P(("col", "row"), None),
    )
    out_specs = (P(("col", "row"), None), P())
    return jax.shard_map(shards, mesh=mesh, in_specs=in_specs, out_specs=out_specs, check_vma=False)
```

profile of v0, /device:TPU:1, one launch (start us, length us, event | category | flops | bytes accessed | tf_op | source)
XLA Modules:
  0.0 596.9 jit_solution(2033896433721760579)
XLA Ops:
  7.2 0.0 copy-start
  7.2 0.0 reduce-scatter.3.cloned.1.call-start
  7.2 0.7 compare_select_fusion
  8.6 38.6 %all_gather.6 = bf16[2048,128]{1,0:T(8,128)(2,1)S(1)} all-gather(bf16[128,128]{1,0:T(8,128)(2,1)} %param.7), channel_id=1, replica_groups=mesh['row'=16,'col'=32] {'row'}, dimensions={0}, use_global_device_ids=true | all-gather | bytes 557056 | tf_op jit(solution)/shard_map/all_gather | solution.py:42
  47.2 7.7 %gather_fusion = bf16[152,128,128]{2,1,0:T(8,128)(2,1)} fusion(bf16[16,128,128]{2,1,0:T(8,128)(2,1)S(1)} %bitcast.46, s32[1024]{0:T(1024)S(1)} %pad_clamp_fusion.2), kind=kCustom, calls=%fused_computation | custom fusion | bytes 9962080 | tf_op jit(solution)/shard_map/gather | solution.py:43
  54.9 11.3 %fusion.4 = f32[152,128,128]{1,2,0:T(8,128)} fusion(bf16[152,128,128]{2,1,0:T(8,128)(2,1)} %gather_fusion, bf16[1,1,152,128,128]{4,3,2,1,0:T(8,128)(2,1)} %param.11), kind=kOutput, calls=%fused_computation.9 | convolution fusion | flops 637534208 | bytes 19922944 | tf_op jit(solution)/shard_map/kij,kjf->kif/dot_general | solution.py:44
  66.3 11.3 %copy.12 = f32[152,128,128]{2,1,0:T(8,128)} copy(f32[152,128,128]{1,2,0:T(8,128)} %fusion.4) | data formatting | bytes 19922944 | tf_op jit(solution)/shard_map/kij,kjf->kif/dot_general | solution.py:44
  77.6 0.2 broadcast_in_dim.17
  77.8 21.0 %scatter_fusion = f32[33,128,128]{2,1,0:T(8,128)S(1)} fusion(f32[33,128,128]{2,1,0:T(8,128)S(1)} %broadcast_in_dim.17, s32[152]{0:T(256)S(1)} %bitcast.51, f32[152,128,128]{2,1,0:T(8,128)} %copy.12), kind=kCustom, calls=%fused_computation.3 | custom fusion | flops 2490368 | bytes 29885024 | tf_op jit(solution)/shard_map/scatter-add | solution.py:25
  98.8 0.0 copy-start.1
  98.8 1.5 slice.14
  100.3 0.0 reduce-scatter.3.cloned.1.call-update
  100.3 0.0 all-gather.2.cloned.1.call-start
  100.4 100.1 %reduce-scatter.3.cloned.1.call-done = f32[128,128]{1,0:T(8,128)} async-done(((f32[4096,128]{1,0:T(8,128)}), f32[128,128]{1,0:T(8,128)}) %reduce-scatter.3.cloned.1.call-update) | async-done | bytes 65552 | tf_op jit(solution)/shard_map/reduce_scatter | solution.py:48
  200.5 0.0 copy-done
  200.5 0.0 copy-done.1
  200.5 1.0 multiply_convert_fusion
  201.5 0.8 convolution_convert_fusion
  202.2 0.0 all-gather.2.cloned.1.call-update
  202.3 0.0 all-reduce.2.cloned.1.call-start
  202.3 1.7 fusion.10
  204.0 0.0 all-reduce.2.cloned.1.call-update
  204.0 0.2 reduce-scatter.5.cloned.1.call-start
  204.2 57.5 %all-gather.2.cloned.1.call-done = bf16[4096,128]{1,0:T(8,128)(2,1)} async-done(((bf16[128,128]{1,0:T(8,128)(2,1)}), bf16[4096,128]{1,0:T(8,128)(2,1)}) %all-gather.2.cloned.1.call-update) | async-done | bytes 1048592 | tf_op jit(solution)/shard_map/all_gather | solution.py:52
  261.7 8.9 %gather_fusion.1 = bf16[152,128,128]{2,1,0:T(8,128)(2,1)} fusion(bf16[32,128,128]{2,1,0:T(8,128)(2,1)} %bitcast.47, s32[1024]{0:T(1024)S(1)} %pad_clamp_fusion.1), kind=kCustom, calls=%fused_computation.1 | custom fusion | bytes 9962080 | tf_op jit(solution)/shard_map/gather | solution.py:54
  270.6 9.5 %fusion.7 = f32[152,128,128]{1,2,0:T(8,128)} fusion(bf16[152,128,128]{2,1,0:T(8,128)(2,1)} %gather_fusion.1, bf16[1,1,152,128,128]{4,3,2,1,0:T(8,128)(2,1)} %param.11), kind=kOutput, calls=%fused_computation.10 | convolution fusion | flops 637534208 | bytes 19922944 | tf_op jit(solution)/shard_map/kij,kif->kjf/dot_general | solution.py:55
  280.2 11.3 %copy.14 = f32[152,128,128]{2,1,0:T(8,128)} copy(f32[152,128,128]{1,2,0:T(8,128)} %fusion.7) | data formatting | bytes 19922944 | tf_op jit(solution)/shard_map/kij,kif->kjf/dot_general | solution.py:55
  291.5 0.1 broadcast_in_dim.16
  291.6 0.0 copy-start.2
  291.6 21.0 %scatter_fusion.1 = f32[17,128,128]{2,1,0:T(8,128)S(1)} fusion(f32[17,128,128]{2,1,0:T(8,128)S(1)} %broadcast_in_dim.16, s32[152]{0:T(256)S(1)} %bitcast.50, f32[152,128,128]{2,1,0:T(8,128)} %copy.14), kind=kCustom, calls=%fused_computation.4 | custom fusion | flops 2490368 | bytes 29885024 | tf_op jit(solution)/shard_map/scatter-add | solution.py:25
  312.6 1.0 slice.15
  313.6 0.0 reduce-scatter.5.cloned.1.call-update
  313.6 0.0 copy-done.2
  313.7 214.6 %all-reduce.2.cloned.1.call-done = f32[128,128]{1,0:T(8,128)} async-done(((f32[128,128]{1,0:T(8,128)}), f32[128,128]{1,0:T(8,128)}) %all-reduce.2.cloned.1.call-update) | async-done | bytes 65552 | tf_op jit(solution)/shard_map/psum | solution.py:53
  528.3 1.5 broadcast_multiply_fusion
  529.8 58.4 %reduce-scatter.5.cloned.1.call-done = f32[128,128]{1,0:T(8,128)} async-done(((f32[2048,128]{1,0:T(8,128)}), f32[128,128]{1,0:T(8,128)}) %reduce-scatter.5.cloned.1.call-update) | async-done | bytes 65552 | tf_op jit(solution)/shard_map/reduce_scatter | solution.py:61
  588.2 0.8 convert_element_type.19
  589.0 1.3 gather_fusion.2
  (5 shorter events, 0.0 us)
Async XLA Ops:
  7.2 193.3 %copy-start = (bf16[128,128]{1,0:T(8,128)(2,1)S(1)}, bf16[128,128]{1,0:T(8,128)(2,1)}, u32[]{:S(2)}) copy-start(bf16[128,128]{1,0:T(8,128)(2,1)} %param.9) | copy-start | bytes 98308
  7.2 193.3 %reduce-scatter.3.cloned.1.call-start = ((), (), s32[]{:S(2)}) async-start(), calls=%async_computation.2 | async-start | bytes 2162688 | tf_op jit(solution)/shard_map/reduce_scatter | solution.py:48
  98.8 101.7 %copy-start.1 = (bf16[128,128]{1,0:T(8,128)(2,1)S(1)}, bf16[128,128]{1,0:T(8,128)(2,1)}, u32[]{:S(2)}) copy-start(bf16[128,128]{1,0:T(8,128)(2,1)} %param.8) | copy-start | bytes 98308
  100.3 161.4 %all-gather.2.cloned.1.call-start = ((), (), s32[]{:S(2)}) async-start(), calls=%async_computation.3 | async-start | bytes 1081344 | tf_op jit(solution)/shard_map/all_gather | solution.py:52
  202.3 326.0 %all-reduce.2.cloned.1.call-start = ((), (), s32[]{:S(2)}) async-start(), calls=%async_computation.5 | async-start | bytes 131072 | tf_op jit(solution)/shard_map/psum | solution.py:53
  204.0 384.1 %reduce-scatter.5.cloned.1.call-start = ((), (), s32[]{:S(2)}) async-start(), calls=%async_computation.4 | async-start | bytes 1114112 | tf_op jit(solution)/shard_map/reduce_scatter | solution.py:61
  291.6 22.0 %copy-start.2 = (s32[1,128]{1,0:T(1,128)S(1)}, s32[1,128]{1,0:T(1,128)}, u32[]{:S(2)}) copy-start(s32[1,128]{1,0:T(1,128)} %param.13) | copy-start | bytes 1540
Sparse Core Ops, SparseCore 0:
  100.4 99.9 reduce-scatter.2
  204.2 57.5 all-gather.1
  267.3 260.9 all-reduce.1
  530.9 57.1 reduce-scatter.4
where the time goes:
time: 609 us; the launch traced here: 597 us
  waiting for transfers between devices  431 us (71%)
  other arithmetic  44.9 us (7%)
  local copies, waits for them, and re-layouts  43.5 us (7%)
  blocking collectives  38.6 us (6%)
  matrix products  24.3 us (4%)
  between operations  14.5 us (2%)
    psum x1, waiting for transfers between devices, shards(): lax.psum(weight_part, ('row', 'col')) * (1.0 / math.sqrt(total_nodes))  215 us
    reduce_scatter x1, waiting for transfers between devices, shards(): lax.psum_scatter(partial_value, 'col', scatter_dimension=0, tiled=True)  100 us
    reduce_scatter x1, waiting for transfers between devices, shards(): lax.psum_scatter(partial_back, 'row', scatter_dimension=0, tiled=True)  58.4 us
    all_gather x1, waiting for transfers between devices, shards(): grad_rows = lax.all_gather(grad_share, 'col', axis=0, tiled=True)  57.5 us
    scatter-add x2, other arithmetic, block_sums(): summed = jax.ops.segment_sum(product, routed, num_segments=segments + 1)  41.9 us
    all_gather x1, blocking collectives, shards(): column_source = lax.all_gather(features, 'row', axis=0, tiled=True)  38.6 us
  transfers between devices with their start and end apart: 4, of which 4 were waited for; matrix products, arithmetic and copies ran while one was open for 9% of the time, Pallas kernels for 0%

commit v1 on v0

v1 whole, which is shorter than its diff:
```python
import math

import jax
import jax.numpy as jnp
from jax import lax
from jax.experimental import pallas as pl
from jax.experimental.pallas import tpu as pltpu
from jax.sharding import PartitionSpec as P

BLOCK = 128
HIDDEN = 128
YL, C, X, YH = 2, 2, 4, 4
CHUNK = 8
MESH = pl.DeviceIdType.MESH
F32, BF16 = jnp.float32, jnp.bfloat16
VMEM = pl.BlockSpec(memory_space=pltpu.VMEM)
SMEM = pl.BlockSpec(memory_space=pltpu.SMEM)
HBM = pl.BlockSpec(memory_space=pl.ANY)


def far_first(n):
    return sorted(range(1, n), key=lambda d: (-min(d, n - d), d))


def near_first(n):
    return sorted(range(1, n), key=lambda d: (min(d, n - d), d))


def remote(src, dst, send, recv, device):
    return pltpu.make_async_remote_copy(
        src_ref=src, dst_ref=dst, send_sem=send, recv_sem=recv, device_id=device, device_id_type=MESH
    )


def greet(devices):
    barrier = pltpu.get_barrier_semaphore()
    for device in devices:
        pl.semaphore_signal(barrier, inc=1, device_id=device, device_id_type=MESH)
    pl.semaphore_wait(barrier, len(devices))


def gather_features(x_ref, out_ref, zs, zr, ys, yr):
    r, c = lax.axis_index("row"), lax.axis_index("col")
    nz = out_ref.shape[0] // YL
    z, y = r // YL, r % YL
    side = (z * YL + 1 - y, c)

    def other(d):
        return ((z + d) % nz * YL + y, c)

    def came(d):
        return (z + nz - d) % nz * YL + y

    greet([side] + [other(d) for d in range(1, nz)])
    sends = []
    for d in near_first(nz):
        copy = remote(x_ref, out_ref.at[r], zs.at[d], zr.at[d], other(d))
        copy.start()
        sends.append(copy)
    copy = remote(x_ref, out_ref.at[r], ys.at[0], yr.at[0], side)
    copy.start()
    sends.append(copy)
    out_ref[r] = x_ref[...]
    for d in near_first(nz):
        at = came(d)
        remote(x_ref, out_ref.at[at], zs.at[d], zr.at[d], other(d)).wait_recv()
        copy = remote(out_ref.at[at], out_ref.at[at], ys.at[d], yr.at[d], side)
        copy.start()
        sends.append(copy)
    for d in range(nz):
        at = (z + nz - d) % nz * YL + 1 - y
        remote(x_ref, out_ref.at[at], ys.at[d], yr.at[d], side).wait_recv()
    for copy in sends:
        copy.wait_send()


def spmm(ids_ref, count_ref, vals_ref, src_ref, out_ref, acc, vbuf, sems, *, cols, forward):
    count = count_ref[0, 0]
    chunks = (count + CHUNK - 1) // CHUNK
    dead = acc.shape[0] - 1

    def fetch(j):
        at = pl.ds(j * CHUNK, CHUNK)
        return pltpu.make_async_copy(vals_ref.at[at], vbuf.at[at], sems.at[j])

    lax.fori_loop(0, chunks, lambda j, _: (fetch(j).start(), 0)[1], 0)
    acc[...] = jnp.zeros_like(acc)

    def step(j, _):
        fetch(j).wait()
        for half in range(0, CHUNK, 4):
            made = []
            for i in range(4):
                k = j * CHUNK + half + i
                where = ids_ref[0, k]
                p, q = where // cols, where % cols
                if forward:
                    got = jnp.dot(vbuf[k], src_ref[q], preferred_element_type=F32)
                    to = p
                else:
                    got = jnp.dot(
                        src_ref[p % C * (src_ref.shape[0] // C) + p // C],
                        vbuf[k],
                        preferred_element_type=F32,
                    )
                    to = q
                made.append((jnp.where(k < count, to, dead), got))
            for to, got in made:
                acc[to] = acc[to] + got
        return 0

    lax.fori_loop(0, chunks, step, 0)
    fast = C if forward else YL
    for b in range(dead):
        out_ref[b % fast * (dead // fast) + b // fast] = acc[b].astype(BF16)


def reduce_and_step(
    part, grad_ref, w_ref, out_ref, wsum_ref,
    sib, sx, rx, sy, ry, share, wpart, wsib, wmine, wx, wy,
    cs, cr, xs, xr, hs, hr, gys, gyr, gxs, gxr, gcs, gcr, wcs, wcr, wxs, wxr, wys, wyr,
):
    r, c = lax.axis_index("row"), lax.axis_index("col")
    core = c % C
    x, h = c // C // YH, c // C % YH
    side = (r, (x * YH + h) * C + 1 - core)

    def at_x(d):
        return (r, ((x + d) % X * YH + h) * C + core)

    def at_h(d):
        return (r, (x * YH + (h + d) % YH) * C + core)

    greet([side] + [at_x(d) for d in range(1, X)] + [at_h(d) for d in range(1, YH)])
    sends = []

    def send(*args):
        copy = remote(*args)
        copy.start()
        sends.append(copy)

    for d in far_first(X) + [0]:
        to = (x + d) % X
        send(part.at[1 - core, to], sib.at[to], cs.at[d], cr.at[d], side)
    for d in far_first(X):
        to = (x + d) % X
        remote(part.at[core, to], sib.at[to], cs.at[d], cr.at[d], side).wait_recv()
        sx[to] = (part[core, to].astype(F32) + sib[to].astype(F32)).astype(BF16)
        send(sx.at[to], rx.at[x], xs.at[d], xr.at[d], at_x(d))
    remote(part.at[core, x], sib.at[x], cs.at[0], cr.at[0], side).wait_recv()
    for d in near_first(X):
        frm = (x + X - d) % X
        remote(sx.at[frm], rx.at[frm], xs.at[d], xr.at[d], at_x(d)).wait_recv()

    def summed(to):
        total = part[core, x, to].astype(F32) + sib[x, to].astype(F32)
        for d in range(1, X):
            total = total + rx[(x + d) % X, to].astype(F32)
        return total

    for d in far_first(YH):
        to = (h + d) % YH
        sy[to] = summed(to).astype(BF16)
        send(sy.at[to], ry.at[h], hs.at[d], hr.at[d], at_h(d))
    aggregate = summed(h)
    for d in near_first(YH):
        frm = (h + YH - d) % YH
        remote(sy.at[frm], ry.at[frm], hs.at[d], hr.at[d], at_h(d)).wait_recv()
    for d in range(1, YH):
        aggregate = aggregate + ry[(h + d) % YH].astype(F32)
    agg_low = aggregate.astype(BF16)
    weight = w_ref[...]
    pre = jnp.dot(agg_low, weight, preferred_element_type=F32)
    sigma = 1.0 / (1.0 + jnp.exp(-pre))
    grad_pre = (grad_ref[...].astype(F32) * sigma * (1.0 + pre * (1.0 - sigma))).astype(BF16)
    flipped = lax.dot_general(weight, grad_pre, (((1,), (1,)), ((), ())), preferred_element_type=F32)
    share[...] = flipped.astype(BF16)
    for d in far_first(YH):
        send(share, out_ref.at[core, x, h], gys.at[d], gyr.at[d], at_h(d))
    for d in far_first(X):
        send(share, out_ref.at[core, x, h], gxs.at[d, 0], gxr.at[d, 0], at_x(d))
    send(share, out_ref.at[core, x, h], gcs.at[0, 0], gcr.at[0, 0], side)
    out_ref[core, x, h] = flipped.astype(BF16)

    half, piece = BLOCK // C, BLOCK // C // X
    wpart[...] = lax.dot_general(
        agg_low, grad_pre, (((0,), (0,)), ((), ())), preferred_element_type=F32
    ).reshape(C, half, HIDDEN)
    send(wpart.at[1 - core], wsib, wcs, wcr, side)
    remote(wpart.at[core], wsib, wcs, wcr, side).wait_recv()
    wmine[...] = (wpart[core] + wsib[...]).reshape(X, piece, HIDDEN)
    for d in far_first(X):
        send(wmine.at[(x + d) % X], wx.at[x], wxs.at[d], wxr.at[d], at_x(d))
    wx[x] = wmine[x]

    for d in near_first(YH):
        block = out_ref.at[core, x, (h + YH - d) % YH]
        remote(share, block, gys.at[d], gyr.at[d], at_h(d)).wait_recv()
        for e in far_first(X):
            send(block, block, gxs.at[e, d], gxr.at[e, d], at_x(e))
        send(block, block, gcs.at[0, d], gcr.at[0, d], side)

    for d in near_first(X):
        frm = (x + X - d) % X
        remote(wmine.at[frm], wx.at[frm], wxs.at[d], wxr.at[d], at_x(d)).wait_recv()
    total = wx[0]
    for s in range(1, X):
        total = total + wx[s]
    wy[h] = total
    for d in far_first(YH):
        send(wy.at[h], wy.at[h], wys.at[d], wyr.at[d], at_h(d))

    for d in [0] + near_first(YH):
        for e in near_first(X):
            block = out_ref.at[core, (x + X - e) % X, (h + YH - d) % YH]
            remote(share, block, gxs.at[e, d], gxr.at[e, d], at_x(e)).wait_recv()
            send(block, block, gcs.at[e, d], gcr.at[e, d], side)

    for d in near_first(YH):
        frm = (h + YH - d) % YH
        remote(wy.at[frm], wy.at[frm], wys.at[d], wyr.at[d], at_h(d)).wait_recv()
    total = wy[0]
    for s in range(1, YH):
        total = total + wy[s]
    wsum_ref[...] = total

    for d in range(YH):
        for e in range(X):
            block = out_ref.at[1 - core, (x + X - e) % X, (h + YH - d) % YH]
            remote(share, block, gcs.at[e, d], gcr.at[e, d], side).wait_recv()
    for copy in sends:
        copy.wait_send()


def reduce_and_order(
    part, perm_ref, wsum_ref, out_ref, wout_ref,
    sib, sz, rz, wside, wz, wall,
    ys, yr, zs, zr, wys, wyr, wzs, wzr, wxs, wxr, wcs, wcr,
    *, scale,
):
    r, c = lax.axis_index("row"), lax.axis_index("col")
    nz = part.shape[1]
    z, y = r // YL, r % YL
    core = c % C
    x, h = c // C // YH, c // C % YH
    side_y = (z * YL + 1 - y, c)
    side_c = (r, (x * YH + h) * C + 1 - core)

    def at_z(d):
        return ((z + d) % nz * YL + y, c)

    def at_x(d):
        return (r, ((x + d) % X * YH + h) * C + core)

    greet(
        [side_y, side_c] + [at_z(d) for d in range(1, nz)] + [at_x(d) for d in range(1, X)]
    )
    sends = []

    def send(*args):
        copy = remote(*args)
        copy.start()
        sends.append(copy)

    send(wsum_ref, wside, wys, wyr, side_y)
    for d in far_first(nz) + [0]:
        to = (z + d) % nz
        send(part.at[1 - y, to], sib.at[to], ys.at[d], yr.at[d], side_y)
    remote(wsum_ref, wside, wys, wyr, side_y).wait_recv()
    wz[z] = wsum_ref[...] + wside[...]
    for d in far_first(nz):
        send(wz.at[z], wz.at[z], wzs.at[d], wzr.at[d], at_z(d))
    for d in far_first(nz):
        to = (z + d) % nz
        remote(part.at[y, to], sib.at[to], ys.at[d], yr.at[d], side_y).wait_recv()
        sz[to] = (part[y, to].astype(F32) + sib[to].astype(F32)).astype(BF16)
        send(sz.at[to], rz.at[z], zs.at[d], zr.at[d], at_z(d))
    remote(part.at[y, z], sib.at[z], ys.at[0], yr.at[0], side_y).wait_recv()
    grad = part[y, z].astype(F32) + sib[z].astype(F32)

    for d in near_first(nz):
        frm = (z + nz - d) % nz
        remote(wz.at[frm], wz.at[frm], wzs.at[d], wzr.at[d], at_z(d)).wait_recv()
    total = wz[0]
    for s in range(1, nz):
        total = total + wz[s]
    wall[core, x] = total * scale
    for d in far_first(X):
        send(wall.at[core, x], wall.at[core, x], wxs.at[d], wxr.at[d], at_x(d))
    for d in near_first(X):
        block = wall.at[core, (x + X - d) % X]
        remote(block, block, wxs.at[d], wxr.at[d], at_x(d)).wait_recv()
    send(wall.at[core], wall.at[core], wcs, wcr, side_c)

    for d in near_first(nz):
        frm = (z + nz - d) % nz
        remote(sz.at[frm], rz.at[frm], zs.at[d], zr.at[d], at_z(d)).wait_recv()
        grad = grad + rz[frm].astype(F32)
    hot = lax.broadcasted_iota(jnp.int32, (BLOCK, BLOCK), 0) == perm_ref[...]
    hot = jnp.where(hot, 1.0, 0.0).astype(BF16)
    moved = jnp.dot(grad.astype(BF16), hot, preferred_element_type=F32)
    out_ref[...] = moved.T.astype(BF16)
    remote(wall.at[1 - core], wall.at[1 - core], wcs, wcr, side_c).wait_recv()
    wout_ref[...] = wall[...].reshape(BLOCK, HIDDEN)
    for copy in sends:
        copy.wait_send()


def dma(*shape):
    return pltpu.SemaphoreType.DMA(shape) if shape else pltpu.SemaphoreType.DMA


def shards(features, grad_out, weight, block_ids, block_vals, block_count, node_perm):
    rows, cols = lax.axis_size("row"), lax.axis_size("col")
    nz = rows // YL
    slots = block_ids.shape[-1]
    blk = (BLOCK, HIDDEN)
    ids, vals = block_ids[0], block_vals[0, 0]
    piece = BLOCK // C // X

    source = pl.pallas_call(
        gather_features,
        out_shape=jax.ShapeDtypeStruct((rows,) + blk, BF16),
        in_specs=[VMEM],
        out_specs=VMEM,
        scratch_shapes=[dma(nz), dma(nz), dma(nz), dma(nz)],
        compiler_params=pltpu.CompilerParams(collective_id=0, has_side_effects=True),
        name="gather_features",
    )(features)

    def multiply(src, targets, forward, name):
        return pl.pallas_call(
            lambda *refs: spmm(*refs, cols=rows, forward=forward),
            out_shape=jax.ShapeDtypeStruct((targets,) + blk, BF16),
            in_specs=[SMEM, SMEM, HBM, VMEM],
            out_specs=VMEM,
            scratch_shapes=[
                pltpu.VMEM((targets + 1,) + blk, F32),
                pltpu.VMEM((slots,) + blk, BF16),
                dma(slots // CHUNK),
            ],
            name=name,
        )(ids, block_count, vals, src)

    part = multiply(source, cols, True, "aggregate").reshape((C, X, YH) + blk)
    grads, wsum = pl.pallas_call(
        reduce_and_step,
        out_shape=(
            jax.ShapeDtypeStruct((C, X, YH) + blk, BF16),
            jax.ShapeDtypeStruct((piece, HIDDEN), F32),
        ),
        in_specs=[VMEM] * 3,
        out_specs=(VMEM, VMEM),
        scratch_shapes=[
            pltpu.VMEM((X, YH) + blk, BF16),
            pltpu.VMEM((X, YH) + blk, BF16),
            pltpu.VMEM((X, YH) + blk, BF16),
            pltpu.VMEM((YH,) + blk, BF16),
            pltpu.VMEM((YH,) + blk, BF16),
            pltpu.VMEM(blk, BF16),
            pltpu.VMEM((C, BLOCK // C, HIDDEN), F32),
            pltpu.VMEM((BLOCK // C, HIDDEN), F32),
            pltpu.VMEM((X, piece, HIDDEN), F32),
            pltpu.VMEM((X, piece, HIDDEN), F32),
            pltpu.VMEM((YH, piece, HIDDEN), F32),
            dma(X), dma(X), dma(X), dma(X), dma(YH), dma(YH),
            dma(YH), dma(YH), dma(X, YH), dma(X, YH), dma(X, YH), dma(X, YH),
            dma(), dma(), dma(X), dma(X), dma(YH), dma(YH),
        ],
        compiler_params=pltpu.CompilerParams(collective_id=1, has_side_effects=True),
        name="reduce_and_step",
    )(part, grad_out, weight)
    back = multiply(grads.reshape((cols,) + blk), rows, False, "aggregate_back")
    scale = 1.0 / math.sqrt(rows * cols * BLOCK)
    return pl.pallas_call(
        lambda *refs: reduce_and_order(*refs, scale=scale),
        out_shape=(jax.ShapeDtypeStruct(blk, BF16), jax.ShapeDtypeStruct((BLOCK, HIDDEN), F32)),
        in_specs=[VMEM] * 3,
        out_specs=(VMEM, VMEM),
        scratch_shapes=[
            pltpu.VMEM((nz,) + blk, BF16),
            pltpu.VMEM((nz,) + blk, BF16),
            pltpu.VMEM((nz,) + blk, BF16),
            pltpu.VMEM((piece, HIDDEN), F32),
            pltpu.VMEM((nz, piece, HIDDEN), F32),
            pltpu.VMEM((C, X, piece, HIDDEN), F32),
            dma(nz), dma(nz), dma(nz), dma(nz), dma(), dma(),
            dma(nz), dma(nz), dma(X), dma(X), dma(), dma(),
        ],
        compiler_params=pltpu.CompilerParams(collective_id=2, has_side_effects=True),
        name="reduce_and_order",
    )(back.reshape((YL, nz) + blk), node_perm, wsum)


def solution(mesh):
    in_specs = (
        P(("col", "row"), None),
        P(("row", "col"), None),
        P(),
        P("row", "col", None),
        P("row", "col", None, None, None),
        P("row", "col"),
        P(("col", "row"), None),
    )
    out_specs = (P(("col", "row"), None), P())
    return jax.shard_map(shards, mesh=mesh, in_specs=in_specs, out_specs=out_specs, check_vma=False)
```

time: 609 us -> 97.2 us (0.16); the launches traced: 597 us -> 96.7 us
  waiting for transfers between devices: 431 us -> 0 us
  Pallas kernels: 0 us -> 92.6 us
  other arithmetic: 44.9 us -> 0 us
  local copies, waits for them, and re-layouts: 43.5 us -> 2.85 us
  blocking collectives: 38.6 us -> 0 us
  matrix products: 24.3 us -> 0 us
  between operations: 14.5 us -> 1.32 us
    psum x1 -> x0, waiting for transfers between devices: 215 us -> none  [shards(): lax.psum(weight_part, ('row', 'col')) * (1.0 / math.sqrt(total_nodes))]
    reduce_scatter x2 -> x0, waiting for transfers between devices: 158 us -> none  [the longest x1 100 us: shards(): lax.psum_scatter(partial_value, 'col', scatter_dimension=0, tiled=True)]
    pallas_call x0 -> x5, Pallas kernels: none -> 92.6 us  [the longest x1 38.1 us: shards(): pl.pallas_call(reduce_and_step, out_shape=(jax.ShapeDtypeStruct((C, X, YH...]
    all_gather x1 -> x0, waiting for transfers between devices: 57.5 us -> none  [shards(): grad_rows = lax.all_gather(grad_share, 'col', axis=0, tiled=True)]
    scatter-add x2 -> x0, other arithmetic: 41.9 us -> none  [block_sums(): summed = jax.ops.segment_sum(product, routed, num_segments=segments + 1)]
    all_gather x1 -> x0, blocking collectives: 38.6 us -> none  [shards(): column_source = lax.all_gather(features, 'row', axis=0, tiled=True)]
    dot_general x5 -> x0, matrix products: 24.3 us -> none  [the longest x1 11.3 us: shards(): jnp.einsum('kij,kjf->kif', values, picked, preferred_element_type=jnp.flo...]
    dot_general x2 -> x0, local copies, waits for them, and re-layouts: 22.6 us -> none  [the longest x1 11.3 us: shards(): jnp.einsum('kij,kif->kjf', values, picked_back, preferred_element_type=jn...]
  transfers between devices with their start and end apart: 4 -> 0, of which waited for: 4 -> 0; matrix products, arithmetic and copies ran while one was open for 9% -> 0% of each run, Pallas kernels for 0% -> 0%
where the time goes in v1:
time: 97.2 us; the launch traced here: 96.7 us
  Pallas kernels  92.6 us (95%)
  local copies, waits for them, and re-layouts  2.85 us (3%)
  between operations  1.32 us (1%)
    pallas_call x1, Pallas kernels, shards(): pl.pallas_call(reduce_and_step, out_shape=(jax.ShapeDtypeStruct((C, X, YH...  38.1 us
    pallas_call x1, Pallas kernels, shards(): pl.pallas_call(lambda *refs: reduce_and_order(*refs, scale=scale), out_sh...  23 us
    pallas_call x1, Pallas kernels, shards(): pl.pallas_call(gather_features, out_shape=jax.ShapeDtypeStruct((rows,) +...  22.6 us
    pallas_call x2, Pallas kernels, multiply(): pl.pallas_call(lambda *refs: spmm(*refs, cols=rows, forward=forward), out...  8.87 us
    unnamed x2, local copies, waits for them, and re-layouts  2.85 us

profile of v1, /device:TPU:1, one launch (start us, length us, event | category | flops | bytes accessed | tf_op | source)
XLA Modules:
  0.0 96.7 jit_solution(17789436188086952182)
XLA Ops:
  1.3 22.6 %gather_features.1.refs_3_ = bf16[16,128,128]{2,1,0:T(8,128)(2,1)} custom-call(bf16[128,128]{1,0:T(8,128)(2,1)} %x_ref.1), custom_call_target="tpu_custom_call" | custom-call | tf_op jit(solution)/shard_map/gather_features/pallas_call | solution.py:321
  23.9 4.4 %aggregate.1 = bf16[32,128,128]{2,1,0:T(8,128)(2,1)} custom-call(s32[1,152]{1,0:T(1,128)} %bitcast.10, s32[1,1]{1,0:T(1,128)S(6)} %copy.11.refs_1_, bf16[152,128,128]{2,1,0:T(8,128)(2,1)} %bitcast.5, bf16[16,128,128]{2,1,0:T(8,128)(2,1)} %gather_features.1.refs_3_), custom_call_target="tpu_custom_call" | custom-call | tf_op jit(solution)/shard_map/aggregate/pallas_call | solution.py:332
  28.3 38.1 %reduce_and_step.1 = (bf16[2,4,4,128,128]{4,3,2,1,0:T(8,128)(2,1)}, f32[16,128]{1,0:T(8,128)}) custom-call(bf16[2,4,4,128,128]{4,3,2,1,0:T(8,128)(2,1)} %bitcast.7, bf16[128,128]{1,0:T(8,128)(2,1)} %grad_ref.1, bf16[128,128]{1,0:T(8,128)(2,1)} %w_ref.1), custom_call_target="tpu_custom_call" | custom-call | tf_op jit(solution)/shard_map/reduce_and_step/pallas_call | solution.py:346
  66.5 4.4 %aggregate_back.1 = bf16[16,128,128]{2,1,0:T(8,128)(2,1)} custom-call(s32[1,152]{1,0:T(1,128)} %bitcast.11, s32[1,1]{1,0:T(1,128)S(6)} %copy.11.refs_1_, bf16[152,128,128]{2,1,0:T(8,128)(2,1)} %bitcast.6, bf16[32,128,128]{2,1,0:T(8,128)(2,1)} %bitcast.9), custom_call_target="tpu_custom_call" | custom-call | tf_op jit(solution)/shard_map/aggregate_back/pallas_call | solution.py:332
  70.9 23.0 %reduce_and_order.1 = (bf16[128,128]{1,0:T(8,128)(2,1)}, f32[128,128]{1,0:T(8,128)}) custom-call(bf16[2,8,128,128]{3,2,1,0:T(8,128)(2,1)} %bitcast.8, s32[1,128]{1,0:T(1,128)} %refs_1_.3, f32[16,128]{1,0:T(8,128)} %get-tuple-element.5.refs_2_), custom_call_target="tpu_custom_call" | custom-call | tf_op jit(solution)/shard_map/reduce_and_order/pallas_call | solution.py:375
  93.9 1.4 %copy.12 = bf16[128,128]{1,0:T(8,128)(2,1)} copy(bf16[128,128]{1,0:T(8,128)(2,1)} %get-tuple-element.8) | data formatting | bytes 65536
  95.3 1.5 %copy.13 = f32[128,128]{1,0:T(8,128)} copy(f32[128,128]{1,0:T(8,128)} %get-tuple-element.9) | data formatting | bytes 131072

commit v2 on v1

v2 whole, which is shorter than its diff:
```python
import math

import jax
import jax.numpy as jnp
from jax import lax
from jax.experimental import pallas as pl
from jax.experimental.pallas import tpu as pltpu
from jax.sharding import PartitionSpec as P

BLOCK = 128
HIDDEN = 128
YL, C, X, YH = 2, 2, 4, 4
CHUNK = 8
LIMIT = 16 << 20
WIDE = 50_000_000
LONG = pl.CostEstimate(flops=0, bytes_accessed=50_000_000, transcendentals=0)
MESH = pl.DeviceIdType.MESH
F32, BF16 = jnp.float32, jnp.bfloat16
VMEM = pl.BlockSpec(memory_space=pltpu.VMEM)
SMEM = pl.BlockSpec(memory_space=pltpu.SMEM)
HBM = pl.BlockSpec(memory_space=pl.ANY)


def far_first(n):
    return sorted(range(1, n), key=lambda d: (-min(d, n - d), d))


def near_first(n):
    return sorted(range(1, n), key=lambda d: (min(d, n - d), d))


def remote(src, dst, send, recv, device):
    return pltpu.make_async_remote_copy(
        src_ref=src, dst_ref=dst, send_sem=send, recv_sem=recv, device_id=device, device_id_type=MESH
    )


def greet(devices):
    barrier = pltpu.get_barrier_semaphore()
    for device in devices:
        pl.semaphore_signal(barrier, inc=1, device_id=device, device_id_type=MESH)
    pl.semaphore_wait(barrier, len(devices))


def spread_along_z(z, nz, turn, at_z, slot, zs, zr, send):
    me = slot(z)
    for d in (2, nz - 2, 1, nz - 1):
        send(me, me, zs.at[d], zr.at[d], at_z(d))

    def arrive(d, sem):
        block = slot((z + nz - d) % nz)
        remote(block, block, zs.at[sem], zr.at[sem], at_z(d)).wait_recv()
        return block

    for d in (1, nz - 1):
        arrive(d, d)
        yield d
    for d in (2, nz - 2):
        block = arrive(d, d)
        onward = 1 if d == 2 else nz - 1
        send(block, block, zs.at[d + 1 if d == 2 else d - 1], zr.at[d + 1 if d == 2 else d - 1], at_z(onward))
        yield d
    back = slot((z + 2 * nz - 2 * turn) % nz)
    send(back, back, zs.at[4], zr.at[4], at_z(2 * nz + 2 * turn))
    for d in (3, nz - 3, 4):
        arrive(d, d)
        yield d


def gather_features(x_ref, vals_ref, out_ref, held_ref, zs, zr, ys, yr, loc, got):
    r, c = lax.axis_index("row"), lax.axis_index("col")
    nz = out_ref.shape[0] // YL
    z, y = r // YL, r % YL
    turn = 1 - 2 * (c % C)
    side = (z * YL + 1 - y, c)

    def at_z(d):
        return ((z + d) % nz * YL + y, c)

    own = pltpu.make_async_copy(x_ref, out_ref.at[r], loc)
    own.start()
    blocks = pltpu.make_async_copy(vals_ref, held_ref, got)
    blocks.start()
    greet([side] + [at_z(d) for d in (1, 2, nz - 2, nz - 1)])
    sends = []

    def send(*args):
        copy = remote(*args)
        copy.start()
        sends.append(copy)

    own.wait()
    send(out_ref.at[r], out_ref.at[r], ys.at[0], yr.at[0], side)
    for d in spread_along_z(z, nz, turn, at_z, lambda at: out_ref.at[at * YL + y], zs, zr, send):
        block = out_ref.at[(z + nz - d) % nz * YL + y]
        send(block, block, ys.at[d], yr.at[d], side)
    for d in range(nz):
        at = (z + nz - d) % nz * YL + 1 - y
        remote(x_ref, out_ref.at[at], ys.at[d], yr.at[d], side).wait_recv()
    for copy in sends:
        copy.wait_send()
    blocks.wait()


def spmm(ids_ref, count_ref, vals_ref, src_ref, out_ref, acc, *, cols, forward):
    count = count_ref[0, 0]
    chunks = (count + CHUNK - 1) // CHUNK
    dead = acc.shape[0] - 1

    acc[...] = jnp.zeros_like(acc)

    def step(j, _):
        for half in range(0, CHUNK, 4):
            made = []
            for i in range(4):
                k = j * CHUNK + half + i
                where = ids_ref[0, k]
                p, q = where // cols, where % cols
                if forward:
                    got = jnp.dot(vals_ref[k], src_ref[q], preferred_element_type=F32)
                    to = p
                else:
                    got = jnp.dot(
                        src_ref[p % C * (src_ref.shape[0] // C) + p // C],
                        vals_ref[k],
                        preferred_element_type=F32,
                    )
                    to = q
                made.append((jnp.where(k < count, to, dead), got))
            for to, got in made:
                acc[to] = acc[to] + got
        return 0

    lax.fori_loop(0, chunks, step, 0)
    fast = C if forward else YL
    for b in range(dead):
        out_ref[b % fast * (dead // fast) + b // fast] = acc[b].astype(BF16)


def reduce_and_step(
    part_ref, grad_ref, w_ref, out_ref, wsum_ref,
    part, sib, sx, rel, rx, sy, ry, share, wpart, wsib, wmine, wx, wy, loc,
    cs, cr, rs, rr, xs, xr, hs, hr, gys, gyr, gxs, gxr, gcs, gcr, wcs, wcr, wxs, wxr, wys, wyr,
):
    r, c = lax.axis_index("row"), lax.axis_index("col")
    core = c % C
    x, h = c // C // YH, c // C % YH
    side = (r, (x * YH + h) * C + 1 - core)

    def at_x(d):
        return (r, ((x + d) % X * YH + h) * C + core)

    def at_h(d):
        return (r, (x * YH + (h + d) % YH) * C + core)

    mine = pltpu.make_async_copy(part_ref.at[core], part, loc)
    mine.start()
    greet([side] + [at_x(d) for d in range(1, X)] + [at_h(d) for d in range(1, YH)])
    sends = []

    def send(*args):
        copy = remote(*args)
        copy.start()
        sends.append(copy)

    def at(e):
        return (h + e) % YH

    for d in (2, 1, 3, 0):
        to = (x + d) % X
        send(part_ref.at[1 - core, to], sib.at[to], cs.at[d], cr.at[d], side)
    mine.wait()

    def have(d):
        to = (x + d) % X
        remote(part.at[to], sib.at[to], cs.at[d], cr.at[d], side).wait_recv()

    def pair(d, e):
        to = (x + d) % X
        return part[to, at(e)].astype(F32) + sib[to, at(e)].astype(F32)

    def push(d, e, total):
        to = (x + d) % X
        sx[to, at(e)] = total.astype(BF16)
        n = 0 if d == 1 else 1
        send(sx.at[to, at(e)], rx.at[n, at(e)], xs.at[n, e], xr.at[n, e], at_x(d))

    ahead = {2: 1, 0: 1, 1: X - 1, 3: X - 1}
    order = (2, 1, 3, 0)
    have(2)
    for e in order:
        sx[(x + 2) % X, at(e)] = pair(2, e).astype(BF16)
        send(sx.at[(x + 2) % X, at(e)], rel.at[at(e)], rs.at[e], rr.at[e], at_x(ahead[e]))
    for d in (1, X - 1):
        have(d)
        for e in order:
            if ahead[e] != d:
                push(d, e, pair(d, e))
    for e in order:
        remote(sx.at[x, at(e)], rel.at[at(e)], rs.at[e], rr.at[e], at_x(1)).wait_recv()
        push(ahead[e], e, pair(ahead[e], e) + rel[at(e)].astype(F32))
    have(0)

    def summed(e):
        for n in (0, 1):
            remote(share, rx.at[n, at(e)], xs.at[n, e], xr.at[n, e], at_x(1)).wait_recv()
        return pair(0, e) + (rx[0, at(e)].astype(F32) + rx[1, at(e)].astype(F32))

    for d in (2, 1, 3):
        to = at(d)
        sy[to] = summed(d).astype(BF16)
        send(sy.at[to], ry.at[h], hs.at[d], hr.at[d], at_h(d))
    aggregate = summed(0)
    for d in near_first(YH):
        frm = (h + YH - d) % YH
        remote(sy.at[frm], ry.at[frm], hs.at[d], hr.at[d], at_h(d)).wait_recv()
    for d in range(1, YH):
        aggregate = aggregate + ry[(h + d) % YH].astype(F32)
    agg_low = aggregate.astype(BF16)
    weight = w_ref[...]
    pre = jnp.dot(agg_low, weight, preferred_element_type=F32)
    sigma = 1.0 / (1.0 + jnp.exp(-pre))
    grad_pre = (grad_ref[...].astype(F32) * sigma * (1.0 + pre * (1.0 - sigma))).astype(BF16)
    flipped = lax.dot_general(weight, grad_pre, (((1,), (1,)), ((), ())), preferred_element_type=F32)
    share[...] = flipped.astype(BF16)
    for d in far_first(YH):
        send(share, out_ref.at[core, x, h], gys.at[d], gyr.at[d], at_h(d))
    for d in (1, X - 1):
        send(share, out_ref.at[core, x, h], gxs.at[d, 0], gxr.at[d, 0], at_x(d))
    send(share, out_ref.at[core, x, h], gcs.at[0, 0], gcr.at[0, 0], side)
    out_ref[core, x, h] = flipped.astype(BF16)

    half, piece = BLOCK // C, BLOCK // C // X
    wpart[...] = lax.dot_general(
        agg_low, grad_pre, (((0,), (0,)), ((), ())), preferred_element_type=F32
    ).reshape(C, half, HIDDEN)
    send(wpart.at[1 - core], wsib, wcs, wcr, side)
    remote(wpart.at[core], wsib, wcs, wcr, side).wait_recv()
    wmine[...] = (wpart[core] + wsib[...]).reshape(X, piece, HIDDEN)
    for d in far_first(X):
        send(wmine.at[(x + d) % X], wx.at[x], wxs.at[d], wxr.at[d], at_x(d))
    wx[x] = wmine[x]

    for d in near_first(YH):
        block = out_ref.at[core, x, (h + YH - d) % YH]
        remote(share, block, gys.at[d], gyr.at[d], at_h(d)).wait_recv()
        for e in (1, X - 1):
            send(block, block, gxs.at[e, d], gxr.at[e, d], at_x(e))
        send(block, block, gcs.at[0, d], gcr.at[0, d], side)

    for d in near_first(X):
        frm = (x + X - d) % X
        remote(wmine.at[frm], wx.at[frm], wxs.at[d], wxr.at[d], at_x(d)).wait_recv()
    total = wx[0]
    for s in range(1, X):
        total = total + wx[s]
    wy[h] = total
    for d in far_first(YH):
        send(wy.at[h], wy.at[h], wys.at[d], wyr.at[d], at_h(d))

    for e in (1, X - 1, 2):
        for d in [0] + near_first(YH):
            block = out_ref.at[core, (x + X - e) % X, (h + YH - d) % YH]
            remote(share, block, gxs.at[e, d], gxr.at[e, d], at_x(e)).wait_recv()
            if e == ahead[d]:
                send(block, block, gxs.at[2, d], gxr.at[2, d], at_x(e))
            send(block, block, gcs.at[e, d], gcr.at[e, d], side)

    for d in near_first(YH):
        frm = (h + YH - d) % YH
        remote(wy.at[frm], wy.at[frm], wys.at[d], wyr.at[d], at_h(d)).wait_recv()
    total = wy[0]
    for s in range(1, YH):
        total = total + wy[s]
    wsum_ref[...] = total

    for d in range(YH):
        for e in range(X):
            block = out_ref.at[1 - core, (x + X - e) % X, (h + YH - d) % YH]
            remote(share, block, gcs.at[e, d], gcr.at[e, d], side).wait_recv()
    for copy in sends:
        copy.wait_send()


def reduce_and_order(
    part_ref, perm_ref, wsum_ref, out_ref, wout_ref,
    part, sib, sz, rel, far, rz, wside, wz, wall, loc,
    ys, yr, rs, rr, fs, fr, zs, zr, wys, wyr, wzs, wzr, wxs, wxr, wcs, wcr,
    *, scale,
):
    r, c = lax.axis_index("row"), lax.axis_index("col")
    nz = part_ref.shape[1]
    z, y = r // YL, r % YL
    core = c % C
    turn = 1 - 2 * core
    x, h = c // C // YH, c // C % YH
    side_y = (z * YL + 1 - y, c)
    side_c = (r, (x * YH + h) * C + 1 - core)

    def at_z(d):
        return ((z + d) % nz * YL + y, c)

    def at_x(d):
        return (r, ((x + d) % X * YH + h) * C + core)

    mine = pltpu.make_async_copy(part_ref.at[y], part, loc)
    mine.start()
    greet(
        [side_y, side_c]
        + [at_z(d) for d in (1, 2, nz - 2, nz - 1)]
        + [at_x(d) for d in range(1, X)]
    )
    sends = []

    def send(*args):
        copy = remote(*args)
        copy.start()
        sends.append(copy)

    send(wsum_ref, wside, wys, wyr, side_y)
    for d in far_first(nz) + [0]:
        to = (z + d) % nz
        send(part_ref.at[1 - y, to], sib.at[to], ys.at[d], yr.at[d], side_y)
    mine.wait()
    remote(wsum_ref, wside, wys, wyr, side_y).wait_recv()
    wz[z] = wsum_ref[...] + wside[...]
    spread = spread_along_z(z, nz, turn, at_z, lambda at: wz.at[at], wzs, wzr, send)
    next(spread)

    def pair(d):
        to = (z + d) % nz
        remote(part.at[to], sib.at[to], ys.at[d], yr.at[d], side_y).wait_recv()
        return part[to].astype(F32) + sib[to].astype(F32)

    def push(d, total, dst, ssem, rsem, device):
        to = (z + d) % nz
        sz[to] = total.astype(BF16)
        send(sz.at[to], dst, ssem, rsem, device)

    push(4, pair(4), far, fs, fr, at_z(2 * nz + 2 * turn))
    for n, d in ((0, 3), (1, nz - 3)):
        push(d, pair(d), rel.at[n], rs.at[n], rr.at[n], at_z(1 if n == 0 else nz - 1))
    two = [pair(2), pair(nz - 2)]
    for n, d in ((2, 1), (3, nz - 1)):
        push(d, pair(d), rz.at[n], zs.at[n], zr.at[n], at_z(d))
    grad = pair(0)
    remote(far, far, fs, fr, side_y).wait_recv()
    beyond = far[...].astype(F32)
    for n, d in ((0, 2), (1, nz - 2)):
        remote(rel.at[n], rel.at[n], rs.at[n], rr.at[n], side_y).wait_recv()
        total = two[n] + rel[n].astype(F32)
        total = total + jnp.where(core == n, beyond, 0.0)
        push(d, total, rz.at[n], zs.at[n], zr.at[n], at_z(d))

    for _ in spread:
        pass
    total = wz[0]
    for s in range(1, nz):
        total = total + wz[s]
    wall[core, x] = total * scale
    for d in far_first(X):
        send(wall.at[core, x], wall.at[core, x], wxs.at[d], wxr.at[d], at_x(d))
    for d in near_first(X):
        block = wall.at[core, (x + X - d) % X]
        remote(block, block, wxs.at[d], wxr.at[d], at_x(d)).wait_recv()
    send(wall.at[core], wall.at[core], wcs, wcr, side_c)

    for n in (2, 3, 0, 1):
        remote(rz.at[n], rz.at[n], zs.at[n], zr.at[n], side_y).wait_recv()
        grad = grad + rz[n].astype(F32)
    hot = lax.broadcasted_iota(jnp.int32, (BLOCK, BLOCK), 0) == perm_ref[...]
    hot = jnp.where(hot, 1.0, 0.0).astype(BF16)
    moved = jnp.dot(grad.astype(BF16), hot, preferred_element_type=F32)
    out_ref[...] = moved.T.astype(BF16)
    remote(wall.at[1 - core], wall.at[1 - core], wcs, wcr, side_c).wait_recv()
    wout_ref[...] = wall[...].reshape(BLOCK, HIDDEN)
    for copy in sends:
        copy.wait_send()


def dma(*shape):
    return pltpu.SemaphoreType.DMA(shape) if shape else pltpu.SemaphoreType.DMA


def shards(features, grad_out, weight, block_ids, block_vals, block_count, node_perm):
    rows, cols = lax.axis_size("row"), lax.axis_size("col")
    nz = rows // YL
    blk = (BLOCK, HIDDEN)
    ids = block_ids[0]
    piece = BLOCK // C // X

    source, vals = pl.pallas_call(
        gather_features,
        out_shape=(
            jax.ShapeDtypeStruct((rows,) + blk, BF16),
            jax.ShapeDtypeStruct(block_vals.shape[2:], BF16),
        ),
        in_specs=[VMEM, pl.BlockSpec(memory_space=pltpu.HBM)],
        out_specs=(VMEM, VMEM),
        scratch_shapes=[dma(nz), dma(nz), dma(nz), dma(nz), dma(), dma()],
        compiler_params=pltpu.CompilerParams(collective_id=0, has_side_effects=True, vmem_limit_bytes=WIDE),
        cost_estimate=LONG,
        name="gather_features",
    )(features, block_vals[0, 0])

    def multiply(src, targets, forward, name):
        return pl.pallas_call(
            lambda *refs: spmm(*refs, cols=rows, forward=forward),
            out_shape=jax.ShapeDtypeStruct((targets,) + blk, BF16),
            in_specs=[SMEM, SMEM, VMEM, VMEM],
            out_specs=VMEM,
            scratch_shapes=[
                pltpu.VMEM((targets + 1,) + blk, F32),
            ],
            compiler_params=pltpu.CompilerParams(vmem_limit_bytes=LIMIT),
            name=name,
        )(ids, block_count, vals, src)

    part = multiply(source, cols, True, "aggregate").reshape((C, X, YH) + blk)
    grads, wsum = pl.pallas_call(
        reduce_and_step,
        out_shape=(
            jax.ShapeDtypeStruct((C, X, YH) + blk, BF16),
            jax.ShapeDtypeStruct((piece, HIDDEN), F32),
        ),
        in_specs=[HBM, VMEM, VMEM],
        out_specs=(VMEM, VMEM),
        scratch_shapes=[
            pltpu.VMEM((X, YH) + blk, BF16),
            pltpu.VMEM((X, YH) + blk, BF16),
            pltpu.VMEM((X, YH) + blk, BF16),
            pltpu.VMEM((YH,) + blk, BF16),
            pltpu.VMEM((2, YH) + blk, BF16),
            pltpu.VMEM((YH,) + blk, BF16),
            pltpu.VMEM((YH,) + blk, BF16),
            pltpu.VMEM(blk, BF16),
            pltpu.VMEM((C, BLOCK // C, HIDDEN), F32),
            pltpu.VMEM((BLOCK // C, HIDDEN), F32),
            pltpu.VMEM((X, piece, HIDDEN), F32),
            pltpu.VMEM((X, piece, HIDDEN), F32),
            pltpu.VMEM((YH, piece, HIDDEN), F32),
            dma(),
            dma(X), dma(X), dma(YH), dma(YH), dma(2, YH), dma(2, YH), dma(YH), dma(YH),
            dma(YH), dma(YH), dma(X, YH), dma(X, YH), dma(X, YH), dma(X, YH),
            dma(), dma(), dma(X), dma(X), dma(YH), dma(YH),
        ],
        compiler_params=pltpu.CompilerParams(collective_id=1, has_side_effects=True, vmem_limit_bytes=LIMIT),
        cost_estimate=LONG,
        name="reduce_and_step",
    )(part, grad_out, weight)
    back = multiply(grads.reshape((cols,) + blk), rows, False, "aggregate_back")
    scale = 1.0 / math.sqrt(rows * cols * BLOCK)
    return pl.pallas_call(
        lambda *refs: reduce_and_order(*refs, scale=scale),
        out_shape=(jax.ShapeDtypeStruct(blk, BF16), jax.ShapeDtypeStruct((BLOCK, HIDDEN), F32)),
        in_specs=[HBM, VMEM, VMEM],
        out_specs=(VMEM, VMEM),
        scratch_shapes=[
            pltpu.VMEM((nz,) + blk, BF16),
            pltpu.VMEM((nz,) + blk, BF16),
            pltpu.VMEM((nz,) + blk, BF16),
            pltpu.VMEM((2,) + blk, BF16),
            pltpu.VMEM(blk, BF16),
            pltpu.VMEM((4,) + blk, BF16),
            pltpu.VMEM((piece, HIDDEN), F32),
            pltpu.VMEM((nz, piece, HIDDEN), F32),
            pltpu.VMEM((C, X, piece, HIDDEN), F32),
            dma(),
            dma(nz), dma(nz), dma(2), dma(2), dma(), dma(), dma(4), dma(4), dma(), dma(),
            dma(nz), dma(nz), dma(X), dma(X), dma(), dma(),
        ],
        compiler_params=pltpu.CompilerParams(collective_id=2, has_side_effects=True, vmem_limit_bytes=LIMIT),
        cost_estimate=LONG,
        name="reduce_and_order",
    )(back.reshape((YL, nz) + blk), node_perm, wsum)


def solution(mesh):
    in_specs = (
        P(("col", "row"), None),
        P(("row", "col"), None),
        P(),
        P("row", "col", None),
        P("row", "col", None, None, None),
        P("row", "col"),
        P(("col", "row"), None),
    )
    out_specs = (P(("col", "row"), None), P())
    return jax.shard_map(shards, mesh=mesh, in_specs=in_specs, out_specs=out_specs, check_vma=False)
```

time: 97.2 us -> 92.8 us (0.955)
  Pallas kernels: 92.6 us -> 89.1 us
    pallas_call x2, Pallas kernels: 8.87 us -> 3.86 us  [multiply(): pl.pallas_call(lambda *refs: spmm(*refs, cols=rows, forward=forward), out...]
    pallas_call x1, Pallas kernels: 23 us -> 27.7 us  [shards(): pl.pallas_call(lambda *refs: reduce_and_order(*refs, scale=scale), out_sh...]
    pallas_call x1, Pallas kernels: 22.6 us -> 20.2 us  [shards(): pl.pallas_call(gather_features, out_shape=(jax.ShapeDtypeStruct((rows,) +...]
    unnamed x2 -> x12, local copies, waits for them, and re-layouts: 2.85 us -> 2.02 us
where the time goes in v2:
time: 92.8 us; the launch traced here: 92.5 us
  Pallas kernels  89.1 us (96%)
  local copies, waits for them, and re-layouts  2.02 us (2%)
  between operations  1.39 us (1%)
    pallas_call x1, Pallas kernels, shards(): pl.pallas_call(reduce_and_step, out_shape=(jax.ShapeDtypeStruct((C, X, YH...  37.3 us
    pallas_call x1, Pallas kernels, shards(): pl.pallas_call(lambda *refs: reduce_and_order(*refs, scale=scale), out_sh...  27.7 us
    pallas_call x1, Pallas kernels, shards(): pl.pallas_call(gather_features, out_shape=(jax.ShapeDtypeStruct((rows,) +...  20.2 us
    pallas_call x2, Pallas kernels, multiply(): pl.pallas_call(lambda *refs: spmm(*refs, cols=rows, forward=forward), out...  3.86 us
    unnamed x12, local copies, waits for them, and re-layouts  2.02 us

profile of v2, /device:TPU:1, one launch (start us, length us, event | category | flops | bytes accessed | tf_op | source)
XLA Modules:
  0.0 92.5 jit_solution(12281370430853572512)
XLA Ops:
  0.6 0.0 copy-start.3
  1.3 0.0 copy-start
  1.3 0.7 copy-done
  2.1 0.0 copy-start.1
  2.1 0.0 copy-start.2
  2.1 20.2 %gather_features.1 = (bf16[16,128,128]{2,1,0:T(8,128)(2,1)S(1)}, bf16[152,128,128]{2,1,0:T(8,128)(2,1)S(1)}) custom-call(bf16[128,128]{1,0:T(8,128)(2,1)S(1)} %copy-done, bf16[152,128,128]{2,1,0:T(8,128)(2,1)} %bitcast.10), custom_call_target="tpu_custom_call" | custom-call | bytes 50000000 | tf_op jit(solution)/shard_map/gather_features/pallas_call | solution.py:392
  22.3 0.0 copy-done.3
  22.3 2.0 %aggregate.1 = bf16[32,128,128]{2,1,0:T(8,128)(2,1)S(1)} custom-call(s32[1,152]{1,0:T(1,128)S(1)} %bitcast.8, s32[1,1]{1,0:T(1,128)S(6)} %copy.11.refs_1_, bf16[152,128,128]{2,1,0:T(8,128)(2,1)S(1)} %get-tuple-element.6.refs_2_, bf16[16,128,128]{2,1,0:T(8,128)(2,1)S(1)} %get-tuple-element.7.refs_3_), custom_call_target="tpu_custom_call" | custom-call | tf_op jit(solution)/shard_map/aggregate/pallas_call | solution.py:407
  24.3 0.0 copy-start.4
  24.3 0.0 copy-done.1
  24.3 0.0 copy-done.2
  24.3 37.3 %reduce_and_step.1 = (bf16[2,4,4,128,128]{4,3,2,1,0:T(8,128)(2,1)S(1)}, f32[16,128]{1,0:T(8,128)S(1)}) custom-call(bf16[2,4,4,128,128]{4,3,2,1,0:T(8,128)(2,1)S(1)} %bitcast.5, bf16[128,128]{1,0:T(8,128)(2,1)S(1)} %copy-done.1, bf16[128,128]{1,0:T(8,128)(2,1)S(1)} %copy-done.2), custom_call_target="tpu_custom_call" | custom-call | bytes 50000000 | tf_op jit(solution)/shard_map/reduce_and_step/pallas_call | solution.py:420
  61.6 1.9 %aggregate_back.1 = bf16[16,128,128]{2,1,0:T(8,128)(2,1)S(1)} custom-call(s32[1,152]{1,0:T(1,128)S(1)} %bitcast.9, s32[1,1]{1,0:T(1,128)S(6)} %copy.11.refs_1_, bf16[152,128,128]{2,1,0:T(8,128)(2,1)S(1)} %get-tuple-element.6.refs_2_, bf16[32,128,128]{2,1,0:T(8,128)(2,1)S(1)} %bitcast.7), custom_call_target="tpu_custom_call" | custom-call | tf_op jit(solution)/shard_map/aggregate_back/pallas_call | solution.py:407
  63.5 0.0 copy-done.4
  63.5 27.7 %reduce_and_order.1 = (bf16[128,128]{1,0:T(8,128)(2,1)S(1)}, f32[128,128]{1,0:T(8,128)S(1)}) custom-call(bf16[2,8,128,128]{3,2,1,0:T(8,128)(2,1)S(1)} %bitcast.6, s32[1,128]{1,0:T(1,128)S(1)} %copy-done.4, f32[16,128]{1,0:T(8,128)S(1)} %get-tuple-element.9.refs_2_), custom_call_target="tpu_custom_call" | custom-call | bytes 50000000 | tf_op jit(solution)/shard_map/reduce_and_order/pallas_call | solution.py:453
  91.2 0.6 copy.12
  91.9 0.6 copy.13
Async XLA Ops:
  0.6 21.6 %copy-start.3 = (s32[1,1,152]{2,1,0:T(1,128)S(1)}, s32[1,1,152]{2,1,0:T(1,128)}, u32[]{:S(2)}) copy-start(s32[1,1,152]{2,1,0:T(1,128)} %param.10) | copy-start | bytes 1828
  1.3 0.8 copy-start
  2.1 22.2 %copy-start.1 = (bf16[128,128]{1,0:T(8,128)(2,1)S(1)}, bf16[128,128]{1,0:T(8,128)(2,1)}, u32[]{:S(2)}) copy-start(bf16[128,128]{1,0:T(8,128)(2,1)} %grad_ref.1) | copy-start | bytes 98308
  2.1 22.2 %copy-start.2 = (bf16[128,128]{1,0:T(8,128)(2,1)S(1)}, bf16[128,128]{1,0:T(8,128)(2,1)}, u32[]{:S(2)}) copy-start(bf16[128,128]{1,0:T(8,128)(2,1)} %w_ref.1) | copy-start | bytes 98308
  24.3 39.2 %copy-start.4 = (s32[1,128]{1,0:T(1,128)S(1)}, s32[1,128]{1,0:T(1,128)}, u32[]{:S(2)}) copy-start(s32[1,128]{1,0:T(1,128)} %refs_1_.3) | copy-start | bytes 1540

commit v3 on v2

--- a/solution.py
+++ b/solution.py
@@ -139,8 +139,8 @@
 
 def reduce_and_step(
     part_ref, grad_ref, w_ref, out_ref, wsum_ref,
-    part, sib, sx, rel, rx, sy, ry, share, wpart, wsib, wmine, wx, wy, loc,
-    cs, cr, rs, rr, xs, xr, hs, hr, gys, gyr, gxs, gxr, gcs, gcr, wcs, wcr, wxs, wxr, wys, wyr,
+    part, sib, sx, rel, rx, sy, ry, share, wpart, wx, wy, loc,
+    cs, cr, rs, rr, xs, xr, hs, hr, gys, gyr, gxs, gxr, gcs, gcr, wxs, wxr, wys, wyr,
 ):
     r, c = lax.axis_index("row"), lax.axis_index("col")
     core = c % C
@@ -153,9 +153,19 @@
     def at_h(d):
         return (r, (x * YH + (h + d) % YH) * C + core)
 
+    z, y = r // YL, r % YL
+
+    def at_xc(f, d):
+        return (r, ((x + d) % X * YH + h) * C + (core + f) % C)
+
+    def at_yh(f, d):
+        return (z * YL + (y + f) % YL, (x * YH + (h + d) % YH) * C + core)
+
+    across = [(f, d) for f in range(C) for d in range(X) if f or d]
+    along = [(f, d) for f in range(YL) for d in range(YH) if f or d]
     mine = pltpu.make_async_copy(part_ref.at[core], part, loc)
     mine.start()
-    greet([side] + [at_x(d) for d in range(1, X)] + [at_h(d) for d in range(1, YH)])
+    greet([at_xc(f, d) for f, d in across] + [at_yh(f, d) for f, d in along])
     sends = []
 
     def send(*args):
@@ -230,16 +240,13 @@
     send(share, out_ref.at[core, x, h], gcs.at[0, 0], gcr.at[0, 0], side)
     out_ref[core, x, h] = flipped.astype(BF16)
 
-    half, piece = BLOCK // C, BLOCK // C // X
     wpart[...] = lax.dot_general(
         agg_low, grad_pre, (((0,), (0,)), ((), ())), preferred_element_type=F32
-    ).reshape(C, half, HIDDEN)
-    send(wpart.at[1 - core], wsib, wcs, wcr, side)
-    remote(wpart.at[core], wsib, wcs, wcr, side).wait_recv()
-    wmine[...] = (wpart[core] + wsib[...]).reshape(X, piece, HIDDEN)
-    for d in far_first(X):
-        send(wmine.at[(x + d) % X], wx.at[x], wxs.at[d], wxr.at[d], at_x(d))
-    wx[x] = wmine[x]
+    ).reshape(wpart.shape)
+    for f, d in across:
+        piece = wpart.at[(core + f) % C, (x + d) % X]
+        send(piece, wx.at[core, x], wxs.at[f, d], wxr.at[f, d], at_xc(f, d))
+    wx[core, x] = wpart[core, x]
 
     for d in near_first(YH):
         block = out_ref.at[core, x, (h + YH - d) % YH]
@@ -248,15 +255,15 @@
             send(block, block, gxs.at[e, d], gxr.at[e, d], at_x(e))
         send(block, block, gcs.at[0, d], gcr.at[0, d], side)
 
-    for d in near_first(X):
-        frm = (x + X - d) % X
-        remote(wmine.at[frm], wx.at[frm], wxs.at[d], wxr.at[d], at_x(d)).wait_recv()
-    total = wx[0]
-    for s in range(1, X):
-        total = total + wx[s]
-    wy[h] = total
-    for d in far_first(YH):
-        send(wy.at[h], wy.at[h], wys.at[d], wyr.at[d], at_h(d))
+    for f, d in across:
+        came = wx.at[(core + f) % C, (x + X - d) % X]
+        remote(came, came, wxs.at[f, d], wxr.at[f, d], at_xc(f, d)).wait_recv()
+    total = wx[0, 0]
+    for n in range(1, C * X):
+        total = total + wx[n // X, n % X]
+    wy[y, h] = total
+    for f, d in along:
+        send(wy.at[y, h], wy.at[y, h], wys.at[f, d], wyr.at[f, d], at_yh(f, d))
 
     for e in (1, X - 1, 2):
         for d in [0] + near_first(YH):
@@ -266,12 +273,12 @@
                 send(block, block, gxs.at[2, d], gxr.at[2, d], at_x(e))
             send(block, block, gcs.at[e, d], gcr.at[e, d], side)
 
-    for d in near_first(YH):
-        frm = (h + YH - d) % YH
-        remote(wy.at[frm], wy.at[frm], wys.at[d], wyr.at[d], at_h(d)).wait_recv()
-    total = wy[0]
-    for s in range(1, YH):
-        total = total + wy[s]
+    for f, d in along:
+        came = wy.at[(y + f) % YL, (h + YH - d) % YH]
+        remote(came, came, wys.at[f, d], wyr.at[f, d], at_yh(f, d)).wait_recv()
+    total = wy[0, 0]
+    for n in range(1, YL * YH):
+        total = total + wy[n // YH, n % YH]
     wsum_ref[...] = total
 
     for d in range(YH):
@@ -284,32 +291,27 @@
 
 def reduce_and_order(
     part_ref, perm_ref, wsum_ref, out_ref, wout_ref,
-    part, sib, sz, rel, far, rz, wside, wz, wall, loc,
-    ys, yr, rs, rr, fs, fr, zs, zr, wys, wyr, wzs, wzr, wxs, wxr, wcs, wcr,
+    part, sib, sz, rz, wz, wall, loc,
+    ys, yr, zs, zr, wzs, wzr, wxs, wxr,
     *, scale,
 ):
     r, c = lax.axis_index("row"), lax.axis_index("col")
     nz = part_ref.shape[1]
     z, y = r // YL, r % YL
     core = c % C
-    turn = 1 - 2 * core
     x, h = c // C // YH, c // C % YH
-    side_y = (z * YL + 1 - y, c)
-    side_c = (r, (x * YH + h) * C + 1 - core)
+    side = (z * YL + 1 - y, c)
 
     def at_z(d):
         return ((z + d) % nz * YL + y, c)
 
-    def at_x(d):
-        return (r, ((x + d) % X * YH + h) * C + core)
-
+    def at_xc(f, d):
+        return (r, ((x + d) % X * YH + h) * C + (core + f) % C)
+
+    across = [(f, d) for f in range(C) for d in range(X) if f or d]
     mine = pltpu.make_async_copy(part_ref.at[y], part, loc)
     mine.start()
-    greet(
-        [side_y, side_c]
-        + [at_z(d) for d in (1, 2, nz - 2, nz - 1)]
-        + [at_x(d) for d in range(1, X)]
-    )
+    greet([side] + [at_z(d) for d in range(1, nz)] + [at_xc(f, d) for f, d in across])
     sends = []
 
     def send(*args):
@@ -317,62 +319,46 @@
         copy.start()
         sends.append(copy)
 
-    send(wsum_ref, wside, wys, wyr, side_y)
     for d in far_first(nz) + [0]:
         to = (z + d) % nz
-        send(part_ref.at[1 - y, to], sib.at[to], ys.at[d], yr.at[d], side_y)
+        send(part_ref.at[1 - y, to], sib.at[to], ys.at[d], yr.at[d], side)
+    for d in far_first(nz):
+        send(wsum_ref, wz.at[z], wzs.at[d], wzr.at[d], at_z(d))
+    wz[z] = wsum_ref[...]
     mine.wait()
-    remote(wsum_ref, wside, wys, wyr, side_y).wait_recv()
-    wz[z] = wsum_ref[...] + wside[...]
-    spread = spread_along_z(z, nz, turn, at_z, lambda at: wz.at[at], wzs, wzr, send)
-    next(spread)
 
     def pair(d):
         to = (z + d) % nz
-        remote(part.at[to], sib.at[to], ys.at[d], yr.at[d], side_y).wait_recv()
+        remote(part.at[to], sib.at[to], ys.at[d], yr.at[d], side).wait_recv()
         return part[to].astype(F32) + sib[to].astype(F32)
 
-    def push(d, total, dst, ssem, rsem, device):
+    for d in far_first(nz):
         to = (z + d) % nz
-        sz[to] = total.astype(BF16)
-        send(sz.at[to], dst, ssem, rsem, device)
-
-    push(4, pair(4), far, fs, fr, at_z(2 * nz + 2 * turn))
-    for n, d in ((0, 3), (1, nz - 3)):
-        push(d, pair(d), rel.at[n], rs.at[n], rr.at[n], at_z(1 if n == 0 else nz - 1))
-    two = [pair(2), pair(nz - 2)]
-    for n, d in ((2, 1), (3, nz - 1)):
-        push(d, pair(d), rz.at[n], zs.at[n], zr.at[n], at_z(d))
+        sz[to] = pair(d).astype(BF16)
+        send(sz.at[to], rz.at[z], zs.at[d], zr.at[d], at_z(d))
     grad = pair(0)
-    remote(far, far, fs, fr, side_y).wait_recv()
-    beyond = far[...].astype(F32)
-    for n, d in ((0, 2), (1, nz - 2)):
-        remote(rel.at[n], rel.at[n], rs.at[n], rr.at[n], side_y).wait_recv()
-        total = two[n] + rel[n].astype(F32)
-        total = total + jnp.where(core == n, beyond, 0.0)
-        push(d, total, rz.at[n], zs.at[n], zr.at[n], at_z(d))
-
-    for _ in spread:
-        pass
+
+    for d in near_first(nz):
+        came = wz.at[(z + nz - d) % nz]
+        remote(came, came, wzs.at[d], wzr.at[d], at_z(d)).wait_recv()
     total = wz[0]
     for s in range(1, nz):
         total = total + wz[s]
     wall[core, x] = total * scale
-    for d in far_first(X):
-        send(wall.at[core, x], wall.at[core, x], wxs.at[d], wxr.at[d], at_x(d))
-    for d in near_first(X):
-        block = wall.at[core, (x + X - d) % X]
-        remote(block, block, wxs.at[d], wxr.at[d], at_x(d)).wait_recv()
-    send(wall.at[core], wall.at[core], wcs, wcr, side_c)
-
-    for n in (2, 3, 0, 1):
-        remote(rz.at[n], rz.at[n], zs.at[n], zr.at[n], side_y).wait_recv()
-        grad = grad + rz[n].astype(F32)
+    for f, d in across:
+        send(wall.at[core, x], wall.at[core, x], wxs.at[f, d], wxr.at[f, d], at_xc(f, d))
+
+    for d in near_first(nz):
+        frm = (z + nz - d) % nz
+        remote(sz.at[frm], rz.at[frm], zs.at[d], zr.at[d], at_z(d)).wait_recv()
+        grad = grad + rz[frm].astype(F32)
     hot = lax.broadcasted_iota(jnp.int32, (BLOCK, BLOCK), 0) == perm_ref[...]
     hot = jnp.where(hot, 1.0, 0.0).astype(BF16)
     moved = jnp.dot(grad.astype(BF16), hot, preferred_element_type=F32)
     out_ref[...] = moved.T.astype(BF16)
-    remote(wall.at[1 - core], wall.at[1 - core], wcs, wcr, side_c).wait_recv()
+    for f, d in across:
+        came = wall.at[(core + f) % C, (x + X - d) % X]
+        remote(came, came, wxs.at[f, d], wxr.at[f, d], at_xc(f, d)).wait_recv()
     wout_ref[...] = wall[...].reshape(BLOCK, HIDDEN)
     for copy in sends:
         copy.wait_send()
@@ -434,15 +420,13 @@
             pltpu.VMEM((YH,) + blk, BF16),
             pltpu.VMEM((YH,) + blk, BF16),
             pltpu.VMEM(blk, BF16),
-            pltpu.VMEM((C, BLOCK // C, HIDDEN), F32),
-            pltpu.VMEM((BLOCK // C, HIDDEN), F32),
-            pltpu.VMEM((X, piece, HIDDEN), F32),
-            pltpu.VMEM((X, piece, HIDDEN), F32),
-            pltpu.VMEM((YH, piece, HIDDEN), F32),
+            pltpu.VMEM((C, X, piece, HIDDEN), F32),
+            pltpu.VMEM((C, X, piece, HIDDEN), F32),
+            pltpu.VMEM((YL, YH, piece, HIDDEN), F32),
             dma(),
             dma(X), dma(X), dma(YH), dma(YH), dma(2, YH), dma(2, YH), dma(YH), dma(YH),
             dma(YH), dma(YH), dma(X, YH), dma(X, YH), dma(X, YH), dma(X, YH),
-            dma(), dma(), dma(X), dma(X), dma(YH), dma(YH),
+            dma(C, X), dma(C, X), dma(YL, YH), dma(YL, YH),
         ],
         compiler_params=pltpu.CompilerParams(collective_id=1, has_side_effects=True, vmem_limit_bytes=LIMIT),
         cost_estimate=LONG,
@@ -459,15 +443,11 @@
             pltpu.VMEM((nz,) + blk, BF16),
             pltpu.VMEM((nz,) + blk, BF16),
             pltpu.VMEM((nz,) + blk, BF16),
-            pltpu.VMEM((2,) + blk, BF16),
-            pltpu.VMEM(blk, BF16),
-            pltpu.VMEM((4,) + blk, BF16),
-            pltpu.VMEM((piece, HIDDEN), F32),
+            pltpu.VMEM((nz,) + blk, BF16),
             pltpu.VMEM((nz, piece, HIDDEN), F32),
             pltpu.VMEM((C, X, piece, HIDDEN), F32),
             dma(),
-            dma(nz), dma(nz), dma(2), dma(2), dma(), dma(), dma(4), dma(4), dma(), dma(),
-            dma(nz), dma(nz), dma(X), dma(X), dma(), dma(),
+            dma(nz), dma(nz), dma(nz), dma(nz), dma(nz), dma(nz), dma(C, X), dma(C, X),
         ],
         compiler_params=pltpu.CompilerParams(collective_id=2, has_side_effects=True, vmem_limit_bytes=LIMIT),
         cost_estimate=LONG,

time: 92.8 us -> 86.7 us (0.934)
  Pallas kernels: 89.1 us -> 83 us
    pallas_call x1, Pallas kernels: 27.7 us -> 17.5 us  [shards(): pl.pallas_call(lambda *refs: reduce_and_order(*refs, scale=scale), out_sh...]
    pallas_call x2, Pallas kernels: 3.86 us -> 9.62 us  [multiply(): pl.pallas_call(lambda *refs: spmm(*refs, cols=rows, forward=forward), out...]
    pallas_call x1, Pallas kernels: 37.3 us -> 35.6 us  [shards(): pl.pallas_call(reduce_and_step, out_shape=(jax.ShapeDtypeStruct((C, X, YH...]
where the time goes in v3:
time: 86.7 us; the launch traced here: 86.4 us
  Pallas kernels  83 us (96%)
  local copies, waits for them, and re-layouts  2.02 us (2%)
  between operations  1.39 us (2%)
    pallas_call x1, Pallas kernels, shards(): pl.pallas_call(reduce_and_step, out_shape=(jax.ShapeDtypeStruct((C, X, YH...  35.6 us
    pallas_call x1, Pallas kernels, shards(): pl.pallas_call(gather_features, out_shape=(jax.ShapeDtypeStruct((rows,) +...  20.2 us
    pallas_call x1, Pallas kernels, shards(): pl.pallas_call(lambda *refs: reduce_and_order(*refs, scale=scale), out_sh...  17.5 us
    pallas_call x2, Pallas kernels, multiply(): pl.pallas_call(lambda *refs: spmm(*refs, cols=rows, forward=forward), out...  9.62 us
    unnamed x12, local copies, waits for them, and re-layouts  2.02 us

profile of v3, /device:TPU:1, one launch (start us, length us, event | category | flops | bytes accessed | tf_op | source)
XLA Modules:
  0.0 86.4 jit_solution(3933212565197721514)
XLA Ops:
  0.6 0.0 copy-start.3
  1.3 0.0 copy-start
  1.3 0.7 copy-done
  2.1 0.0 copy-start.1
  2.1 0.0 copy-start.2
  2.1 20.2 %gather_features.1 = (bf16[16,128,128]{2,1,0:T(8,128)(2,1)S(1)}, bf16[152,128,128]{2,1,0:T(8,128)(2,1)S(1)}) custom-call(bf16[128,128]{1,0:T(8,128)(2,1)S(1)} %copy-done, bf16[152,128,128]{2,1,0:T(8,128)(2,1)} %bitcast.10), custom_call_target="tpu_custom_call" | custom-call | bytes 50000000 | tf_op jit(solution)/shard_map/gather_features/pallas_call | solution.py:378
  22.3 0.0 copy-done.3
  22.3 4.8 %aggregate.1 = bf16[32,128,128]{2,1,0:T(8,128)(2,1)S(1)} custom-call(s32[1,152]{1,0:T(1,128)S(1)} %bitcast.8, s32[1,1]{1,0:T(1,128)S(6)} %copy.11.refs_1_, bf16[152,128,128]{2,1,0:T(8,128)(2,1)S(1)} %get-tuple-element.6.refs_2_, bf16[16,128,128]{2,1,0:T(8,128)(2,1)S(1)} %get-tuple-element.7.refs_3_), custom_call_target="tpu_custom_call" | custom-call | tf_op jit(solution)/shard_map/aggregate/pallas_call | solution.py:393
  27.1 0.0 copy-start.4
  27.1 0.0 copy-done.1
  27.1 0.0 copy-done.2
  27.1 35.6 %reduce_and_step.1 = (bf16[2,4,4,128,128]{4,3,2,1,0:T(8,128)(2,1)S(1)}, f32[16,128]{1,0:T(8,128)S(1)}) custom-call(bf16[2,4,4,128,128]{4,3,2,1,0:T(8,128)(2,1)S(1)} %bitcast.5, bf16[128,128]{1,0:T(8,128)(2,1)S(1)} %copy-done.1, bf16[128,128]{1,0:T(8,128)(2,1)S(1)} %copy-done.2), custom_call_target="tpu_custom_call" | custom-call | bytes 50000000 | tf_op jit(solution)/shard_map/reduce_and_step/pallas_call | solution.py:406
  62.8 4.8 %aggregate_back.1 = bf16[16,128,128]{2,1,0:T(8,128)(2,1)S(1)} custom-call(s32[1,152]{1,0:T(1,128)S(1)} %bitcast.9, s32[1,1]{1,0:T(1,128)S(6)} %copy.11.refs_1_, bf16[152,128,128]{2,1,0:T(8,128)(2,1)S(1)} %get-tuple-element.6.refs_2_, bf16[32,128,128]{2,1,0:T(8,128)(2,1)S(1)} %bitcast.7), custom_call_target="tpu_custom_call" | custom-call | tf_op jit(solution)/shard_map/aggregate_back/pallas_call | solution.py:393
  67.6 0.0 copy-done.4
  67.6 17.5 %reduce_and_order.1 = (bf16[128,128]{1,0:T(8,128)(2,1)S(1)}, f32[128,128]{1,0:T(8,128)S(1)}) custom-call(bf16[2,8,128,128]{3,2,1,0:T(8,128)(2,1)S(1)} %bitcast.6, s32[1,128]{1,0:T(1,128)S(1)} %copy-done.4, f32[16,128]{1,0:T(8,128)S(1)} %get-tuple-element.9.refs_2_), custom_call_target="tpu_custom_call" | custom-call | bytes 50000000 | tf_op jit(solution)/shard_map/reduce_and_order/pallas_call | solution.py:437
  85.1 0.6 copy.12
  85.7 0.6 copy.13
Async XLA Ops:
  0.6 21.6 %copy-start.3 = (s32[1,1,152]{2,1,0:T(1,128)S(1)}, s32[1,1,152]{2,1,0:T(1,128)}, u32[]{:S(2)}) copy-start(s32[1,1,152]{2,1,0:T(1,128)} %param.10) | copy-start | bytes 1828
  1.3 0.8 copy-start
  2.1 25.1 %copy-start.1 = (bf16[128,128]{1,0:T(8,128)(2,1)S(1)}, bf16[128,128]{1,0:T(8,128)(2,1)}, u32[]{:S(2)}) copy-start(bf16[128,128]{1,0:T(8,128)(2,1)} %grad_ref.1) | copy-start | bytes 98308
  2.1 25.1 %copy-start.2 = (bf16[128,128]{1,0:T(8,128)(2,1)S(1)}, bf16[128,128]{1,0:T(8,128)(2,1)}, u32[]{:S(2)}) copy-start(bf16[128,128]{1,0:T(8,128)(2,1)} %w_ref.1) | copy-start | bytes 98308
  27.1 40.5 %copy-start.4 = (s32[1,128]{1,0:T(1,128)S(1)}, s32[1,128]{1,0:T(1,128)}, u32[]{:S(2)}) copy-start(s32[1,128]{1,0:T(1,128)} %refs_1_.3) | copy-start | bytes 1540

commit v4 on v3

--- a/solution.py
+++ b/solution.py
@@ -102,45 +102,61 @@
     blocks.wait()
 
 
-def spmm(ids_ref, count_ref, vals_ref, src_ref, out_ref, acc, *, cols, forward):
-    count = count_ref[0, 0]
-    chunks = (count + CHUNK - 1) // CHUNK
+def multiply(ids_ref, count_ref, vals_ref, src_ref, out_ref, tab_ref, last_ref, acc, spot, head):
+    count, cols, slots = count_ref[0, 0], src_ref.shape[0], ids_ref.shape[1]
     dead = acc.shape[0] - 1
-
     acc[...] = jnp.zeros_like(acc)
+    for q in range(cols):
+        spot[q] = 0
 
     def step(j, _):
         for half in range(0, CHUNK, 4):
             made = []
             for i in range(4):
                 k = j * CHUNK + half + i
-                where = ids_ref[0, k]
-                p, q = where // cols, where % cols
-                if forward:
-                    got = jnp.dot(vals_ref[k], src_ref[q], preferred_element_type=F32)
-                    to = p
-                else:
-                    got = jnp.dot(
-                        src_ref[p % C * (src_ref.shape[0] // C) + p // C],
-                        vals_ref[k],
-                        preferred_element_type=F32,
-                    )
-                    to = q
-                made.append((jnp.where(k < count, to, dead), got))
+                p, q = ids_ref[0, k] // cols, ids_ref[0, k] % cols
+                spot[q] = spot[q] + jnp.where(k < count, 1, 0)
+                got = jnp.dot(vals_ref[k], src_ref[q], preferred_element_type=F32)
+                made.append((jnp.where(k < count, p, dead), got))
             for to, got in made:
                 acc[to] = acc[to] + got
         return 0
 
-    lax.fori_loop(0, chunks, step, 0)
-    fast = C if forward else YL
+    lax.fori_loop(0, (count + CHUNK - 1) // CHUNK, step, 0)
+    begin = jnp.int32(0)
+    for q in range(cols):
+        n = spot[q]
+        spot[q] = begin
+        head[q] = begin
+        begin = begin + n
+        last_ref[0, q] = jnp.where(n > 0, begin - 1, slots)
+
+    def place(k, _):
+        p, q = ids_ref[0, k] // cols, ids_ref[0, k] % cols
+        at = spot[q]
+        spot[q] = at + 1
+        tab_ref[0, at] = k
+        tab_ref[1, at] = p % C * (dead // C) + p // C
+        tab_ref[2, at] = jnp.where(at == head[q], 0, 1)
+        return 0
+
+    def blank(k, _):
+        for n in range(3):
+            tab_ref[n, k] = 0
+        return 0
+
+    lax.fori_loop(0, count, place, 0)
+    lax.fori_loop(count, slots, blank, 0)
     for b in range(dead):
-        out_ref[b % fast * (dead // fast) + b // fast] = acc[b].astype(BF16)
-
-
-def reduce_and_step(
-    part_ref, grad_ref, w_ref, out_ref, wsum_ref,
-    part, sib, sx, rel, rx, sy, ry, share, wpart, wx, wy, loc,
+        out_ref[b % C * (dead // C) + b // C] = acc[b].astype(BF16)
+
+
+def reduce_step_and_back(
+    part_ref, grad_ref, w_ref, tab_ref, last_ref, vals_ref, perm_ref, out_ref, wout_ref,
+    part, sib, sx, rel, rx, sy, ry, share, wpart, wx, wy, grads, sums, back, zsib, sz, rz, wz, wall, loc,
     cs, cr, rs, rr, xs, xr, hs, hr, gys, gyr, gxs, gxr, gcs, gcr, wxs, wxr, wys, wyr,
+    ys, yr, zs, zr, wzs, wzr, was, war,
+    *, scale,
 ):
     r, c = lax.axis_index("row"), lax.axis_index("col")
     core = c % C
@@ -165,7 +181,20 @@
     along = [(f, d) for f in range(YL) for d in range(YH) if f or d]
     mine = pltpu.make_async_copy(part_ref.at[core], part, loc)
     mine.start()
-    greet([at_xc(f, d) for f, d in across] + [at_yh(f, d) for f, d in along])
+    nz = zsib.shape[0]
+    side_y = at_yh(1, 0)
+
+    def at_z(d):
+        return ((z + d) % nz * YL + y, c)
+
+    def shared(core, x, h):
+        return grads.at[(core * X + x) * YH + h]
+
+    greet(
+        [at_xc(f, d) for f, d in across]
+        + [at_yh(f, d) for f, d in along]
+        + [at_z(d) for d in range(1, nz)]
+    )
     sends = []
 
     def send(*args):
@@ -234,11 +263,11 @@
     flipped = lax.dot_general(weight, grad_pre, (((1,), (1,)), ((), ())), preferred_element_type=F32)
     share[...] = flipped.astype(BF16)
     for d in far_first(YH):
-        send(share, out_ref.at[core, x, h], gys.at[d], gyr.at[d], at_h(d))
+        send(share, shared(core, x, h), gys.at[d], gyr.at[d], at_h(d))
     for d in (1, X - 1):
-        send(share, out_ref.at[core, x, h], gxs.at[d, 0], gxr.at[d, 0], at_x(d))
-    send(share, out_ref.at[core, x, h], gcs.at[0, 0], gcr.at[0, 0], side)
-    out_ref[core, x, h] = flipped.astype(BF16)
+        send(share, shared(core, x, h), gxs.at[d, 0], gxr.at[d, 0], at_x(d))
+    send(share, shared(core, x, h), gcs.at[0, 0], gcr.at[0, 0], side)
+    grads[(core * X + x) * YH + h] = flipped.astype(BF16)
 
     wpart[...] = lax.dot_general(
         agg_low, grad_pre, (((0,), (0,)), ((), ())), preferred_element_type=F32
@@ -249,7 +278,7 @@
     wx[core, x] = wpart[core, x]
 
     for d in near_first(YH):
-        block = out_ref.at[core, x, (h + YH - d) % YH]
+        block = shared(core, x, (h + YH - d) % YH)
         remote(share, block, gys.at[d], gyr.at[d], at_h(d)).wait_recv()
         for e in (1, X - 1):
             send(block, block, gxs.at[e, d], gxr.at[e, d], at_x(e))
@@ -267,7 +296,7 @@
 
     for e in (1, X - 1, 2):
         for d in [0] + near_first(YH):
-            block = out_ref.at[core, (x + X - e) % X, (h + YH - d) % YH]
+            block = shared(core, (x + X - e) % X, (h + YH - d) % YH)
             remote(share, block, gxs.at[e, d], gxr.at[e, d], at_x(e)).wait_recv()
             if e == ahead[d]:
                 send(block, block, gxs.at[2, d], gxr.at[2, d], at_x(e))
@@ -279,64 +308,41 @@
     total = wy[0, 0]
     for n in range(1, YL * YH):
         total = total + wy[n // YH, n % YH]
-    wsum_ref[...] = total
+    wz[z] = total
+    for d in far_first(nz):
+        send(wz.at[z], wz.at[z], wzs.at[d], wzr.at[d], at_z(d))
 
     for d in range(YH):
         for e in range(X):
-            block = out_ref.at[1 - core, (x + X - e) % X, (h + YH - d) % YH]
+            block = shared(1 - core, (x + X - e) % X, (h + YH - d) % YH)
             remote(share, block, gcs.at[e, d], gcr.at[e, d], side).wait_recv()
-    for copy in sends:
-        copy.wait_send()
-
-
-def reduce_and_order(
-    part_ref, perm_ref, wsum_ref, out_ref, wout_ref,
-    part, sib, sz, rz, wz, wall, loc,
-    ys, yr, zs, zr, wzs, wzr, wxs, wxr,
-    *, scale,
-):
-    r, c = lax.axis_index("row"), lax.axis_index("col")
-    nz = part_ref.shape[1]
-    z, y = r // YL, r % YL
-    core = c % C
-    x, h = c // C // YH, c // C % YH
-    side = (z * YL + 1 - y, c)
-
-    def at_z(d):
-        return ((z + d) % nz * YL + y, c)
-
-    def at_xc(f, d):
-        return (r, ((x + d) % X * YH + h) * C + (core + f) % C)
-
-    across = [(f, d) for f in range(C) for d in range(X) if f or d]
-    mine = pltpu.make_async_copy(part_ref.at[y], part, loc)
-    mine.start()
-    greet([side] + [at_z(d) for d in range(1, nz)] + [at_xc(f, d) for f, d in across])
-    sends = []
-
-    def send(*args):
-        copy = remote(*args)
-        copy.start()
-        sends.append(copy)
-
+
+    sums[sums.shape[0] - 1] = jnp.zeros((BLOCK, HIDDEN), F32)
+
+    def step(j, acc):
+        for i in range(CHUNK):
+            k = j * CHUNK + i
+            got = jnp.dot(grads[tab_ref[1, k]], vals_ref[tab_ref[0, k]], preferred_element_type=F32)
+            acc = acc * tab_ref[2, k].astype(F32) + got
+            sums[k] = acc
+        return acc
+
+    lax.fori_loop(0, (sums.shape[0] - 1) // CHUNK, step, jnp.zeros((BLOCK, HIDDEN), F32))
     for d in far_first(nz) + [0]:
         to = (z + d) % nz
-        send(part_ref.at[1 - y, to], sib.at[to], ys.at[d], yr.at[d], side)
-    for d in far_first(nz):
-        send(wsum_ref, wz.at[z], wzs.at[d], wzr.at[d], at_z(d))
-    wz[z] = wsum_ref[...]
-    mine.wait()
-
-    def pair(d):
+        back[to] = sums[last_ref[0, to * YL + 1 - y]].astype(BF16)
+        send(back.at[to], zsib.at[to], ys.at[d], yr.at[d], side_y)
+
+    def both(d):
         to = (z + d) % nz
-        remote(part.at[to], sib.at[to], ys.at[d], yr.at[d], side).wait_recv()
-        return part[to].astype(F32) + sib[to].astype(F32)
+        remote(back.at[to], zsib.at[to], ys.at[d], yr.at[d], side_y).wait_recv()
+        return sums[last_ref[0, to * YL + y]] + zsib[to].astype(F32)
 
     for d in far_first(nz):
         to = (z + d) % nz
-        sz[to] = pair(d).astype(BF16)
+        sz[to] = both(d).astype(BF16)
         send(sz.at[to], rz.at[z], zs.at[d], zr.at[d], at_z(d))
-    grad = pair(0)
+    grad = both(0)
 
     for d in near_first(nz):
         came = wz.at[(z + nz - d) % nz]
@@ -346,7 +352,7 @@
         total = total + wz[s]
     wall[core, x] = total * scale
     for f, d in across:
-        send(wall.at[core, x], wall.at[core, x], wxs.at[f, d], wxr.at[f, d], at_xc(f, d))
+        send(wall.at[core, x], wall.at[core, x], was.at[f, d], war.at[f, d], at_xc(f, d))
 
     for d in near_first(nz):
         frm = (z + nz - d) % nz
@@ -358,7 +364,7 @@
     out_ref[...] = moved.T.astype(BF16)
     for f, d in across:
         came = wall.at[(core + f) % C, (x + X - d) % X]
-        remote(came, came, wxs.at[f, d], wxr.at[f, d], at_xc(f, d)).wait_recv()
+        remote(came, came, was.at[f, d], war.at[f, d], at_xc(f, d)).wait_recv()
     wout_ref[...] = wall[...].reshape(BLOCK, HIDDEN)
     for copy in sends:
         copy.wait_send()
@@ -389,27 +395,29 @@
         name="gather_features",
     )(features, block_vals[0, 0])
 
-    def multiply(src, targets, forward, name):
-        return pl.pallas_call(
-            lambda *refs: spmm(*refs, cols=rows, forward=forward),
-            out_shape=jax.ShapeDtypeStruct((targets,) + blk, BF16),
-            in_specs=[SMEM, SMEM, VMEM, VMEM],
-            out_specs=VMEM,
-            scratch_shapes=[
-                pltpu.VMEM((targets + 1,) + blk, F32),
-            ],
-            compiler_params=pltpu.CompilerParams(vmem_limit_bytes=LIMIT),
-            name=name,
-        )(ids, block_count, vals, src)
-
-    part = multiply(source, cols, True, "aggregate").reshape((C, X, YH) + blk)
-    grads, wsum = pl.pallas_call(
-        reduce_and_step,
+    slots = block_ids.shape[-1]
+    part, table, last = pl.pallas_call(
+        multiply,
         out_shape=(
-            jax.ShapeDtypeStruct((C, X, YH) + blk, BF16),
-            jax.ShapeDtypeStruct((piece, HIDDEN), F32),
+            jax.ShapeDtypeStruct((cols,) + blk, BF16),
+            jax.ShapeDtypeStruct((3, slots), jnp.int32),
+            jax.ShapeDtypeStruct((1, rows), jnp.int32),
         ),
-        in_specs=[HBM, VMEM, VMEM],
+        in_specs=[SMEM, SMEM, VMEM, VMEM],
+        out_specs=(VMEM, SMEM, SMEM),
+        scratch_shapes=[
+            pltpu.VMEM((cols + 1,) + blk, F32),
+            pltpu.SMEM((rows,), jnp.int32),
+            pltpu.SMEM((rows,), jnp.int32),
+        ],
+        compiler_params=pltpu.CompilerParams(vmem_limit_bytes=LIMIT),
+        name="aggregate",
+    )(ids, block_count, vals, source)
+    scale = 1.0 / math.sqrt(rows * cols * BLOCK)
+    return pl.pallas_call(
+        lambda *refs: reduce_step_and_back(*refs, scale=scale),
+        out_shape=(jax.ShapeDtypeStruct(blk, BF16), jax.ShapeDtypeStruct((BLOCK, HIDDEN), F32)),
+        in_specs=[HBM, VMEM, VMEM, SMEM, SMEM, VMEM, VMEM],
         out_specs=(VMEM, VMEM),
         scratch_shapes=[
             pltpu.VMEM((X, YH) + blk, BF16),
@@ -423,23 +431,8 @@
             pltpu.VMEM((C, X, piece, HIDDEN), F32),
             pltpu.VMEM((C, X, piece, HIDDEN), F32),
             pltpu.VMEM((YL, YH, piece, HIDDEN), F32),
-            dma(),
-            dma(X), dma(X), dma(YH), dma(YH), dma(2, YH), dma(2, YH), dma(YH), dma(YH),
-            dma(YH), dma(YH), dma(X, YH), dma(X, YH), dma(X, YH), dma(X, YH),
-            dma(C, X), dma(C, X), dma(YL, YH), dma(YL, YH),
-        ],
-        compiler_params=pltpu.CompilerParams(collective_id=1, has_side_effects=True, vmem_limit_bytes=LIMIT),
-        cost_estimate=LONG,
-        name="reduce_and_step",
-    )(part, grad_out, weight)
-    back = multiply(grads.reshape((cols,) + blk), rows, False, "aggregate_back")
-    scale = 1.0 / math.sqrt(rows * cols * BLOCK)
-    return pl.pallas_call(
-        lambda *refs: reduce_and_order(*refs, scale=scale),
-        out_shape=(jax.ShapeDtypeStruct(blk, BF16), jax.ShapeDtypeStruct((BLOCK, HIDDEN), F32)),
-        in_specs=[HBM, VMEM, VMEM],
-        out_specs=(VMEM, VMEM),
-        scratch_shapes=[
+            pltpu.VMEM((cols,) + blk, BF16),
+            pltpu.VMEM((slots + 1,) + blk, F32),
             pltpu.VMEM((nz,) + blk, BF16),
             pltpu.VMEM((nz,) + blk, BF16),
             pltpu.VMEM((nz,) + blk, BF16),
@@ -447,12 +440,17 @@
             pltpu.VMEM((nz, piece, HIDDEN), F32),
             pltpu.VMEM((C, X, piece, HIDDEN), F32),
             dma(),
+            dma(X), dma(X), dma(YH), dma(YH), dma(2, YH), dma(2, YH), dma(YH), dma(YH),
+            dma(YH), dma(YH), dma(X, YH), dma(X, YH), dma(X, YH), dma(X, YH),
+            dma(C, X), dma(C, X), dma(YL, YH), dma(YL, YH),
             dma(nz), dma(nz), dma(nz), dma(nz), dma(nz), dma(nz), dma(C, X), dma(C, X),
         ],
-        compiler_params=pltpu.CompilerParams(collective_id=2, has_side_effects=True, vmem_limit_bytes=LIMIT),
+        compiler_params=pltpu.CompilerParams(
+            collective_id=1, has_side_effects=True, vmem_limit_bytes=24 << 20
+        ),
         cost_estimate=LONG,
-        name="reduce_and_order",
-    )(back.reshape((YL, nz) + blk), node_perm, wsum)
+        name="reduce_step_and_back",
+    )(part.reshape((C, X, YH) + blk), grad_out, weight, table, last, vals, node_perm)
 
 
 def solution(mesh):

time: 86.7 us -> 85.7 us (0.988)
  Pallas kernels: 83 us -> 82 us
    pallas_call x4 -> x2, Pallas kernels: 62.8 us -> 61.8 us  [the longest x1 53.2 us: shards(): pl.pallas_call(lambda *refs: reduce_step_and_back(*refs, scale=scale), ou...]
where the time goes in v4:
time: 85.7 us; the launch traced here: 85.4 us
  Pallas kernels  82 us (96%)
  local copies, waits for them, and re-layouts  2.01 us (2%)
  between operations  1.36 us (2%)
    pallas_call x1, Pallas kernels, shards(): pl.pallas_call(lambda *refs: reduce_step_and_back(*refs, scale=scale), ou...  53.2 us
    pallas_call x1, Pallas kernels, shards(): pl.pallas_call(gather_features, out_shape=(jax.ShapeDtypeStruct((rows,) +...  20.2 us
    pallas_call x1, Pallas kernels, shards(): pl.pallas_call(multiply, out_shape=(jax.ShapeDtypeStruct((cols,) + blk, B...  8.63 us
    unnamed x12, local copies, waits for them, and re-layouts  2.01 us

profile of v4, /device:TPU:1, one launch (start us, length us, event | category | flops | bytes accessed | tf_op | source)
XLA Modules:
  0.0 85.4 jit_solution(6044649505159934139)
XLA Ops:
  0.6 0.0 copy-start.3
  1.3 0.0 copy-start
  1.3 0.7 copy-done
  2.1 0.0 copy-start.1
  2.1 0.0 copy-start.2
  2.1 0.0 copy-start.4
  2.1 20.2 %gather_features.1 = (bf16[16,128,128]{2,1,0:T(8,128)(2,1)S(1)}, bf16[152,128,128]{2,1,0:T(8,128)(2,1)S(1)}) custom-call(bf16[128,128]{1,0:T(8,128)(2,1)S(1)} %copy-done, bf16[152,128,128]{2,1,0:T(8,128)(2,1)} %bitcast.5), custom_call_target="tpu_custom_call" | custom-call | bytes 50000000 | tf_op jit(solution)/shard_map/gather_features/pallas_call | solution.py:384
  22.3 0.0 copy-done.3
  22.3 8.6 %aggregate.1 = (bf16[32,128,128]{2,1,0:T(8,128)(2,1)S(1)}, s32[3,152]{1,0:T(4,128)S(1)}, s32[1,16]{1,0:T(1,128)S(1)}) custom-call(s32[1,152]{1,0:T(1,128)S(1)} %bitcast.4, s32[1,1]{1,0:T(1,128)S(6)} %copy.11.count_ref, bf16[152,128,128]{2,1,0:T(8,128)(2,1)S(1)} %get-tuple-element.7.vals_ref.refs_5_, bf16[16,128,128]{2,1,0:T(8,128)(2,1)S(1)} %get-tuple-element.8.src_ref), custom_call_target="tpu_custom_call" | custom-call | tf_op jit(solution)/shard_map/aggregate/pallas_call | solution.py:399
  30.9 0.0 copy-done.1
  30.9 0.0 copy-done.2
  30.9 0.0 copy-done.4
  30.9 53.2 %reduce_step_and_back.1 = (bf16[128,128]{1,0:T(8,128)(2,1)S(1)}, f32[128,128]{1,0:T(8,128)S(1)}) custom-call(bf16[2,4,4,128,128]{4,3,2,1,0:T(8,128)(2,1)S(1)} %bitcast.3, bf16[128,128]{1,0:T(8,128)(2,1)S(1)} %copy-done.1, bf16[128,128]{1,0:T(8,128)(2,1)S(1)} %copy-done.2, s32[3,152]{1,0:T(4,128)S(1)} %get-tuple-element.10.refs_3_, ...), custom_call_target="tpu_custom_call" | custom-call | bytes 50000000 | tf_op jit(solution)/shard_map/reduce_step_and_back/pallas_call | solution.py:417
  84.1 0.6 copy.12
  84.7 0.6 copy.13
Async XLA Ops:
  0.6 21.6 %copy-start.3 = (s32[1,1,152]{2,1,0:T(1,128)S(1)}, s32[1,1,152]{2,1,0:T(1,128)}, u32[]{:S(2)}) copy-start(s32[1,1,152]{2,1,0:T(1,128)} %param.10) | copy-start | bytes 1828
  1.3 0.8 copy-start
  2.1 28.9 %copy-start.1 = (bf16[128,128]{1,0:T(8,128)(2,1)S(1)}, bf16[128,128]{1,0:T(8,128)(2,1)}, u32[]{:S(2)}) copy-start(bf16[128,128]{1,0:T(8,128)(2,1)} %refs_1_.1) | copy-start | bytes 98308
  2.1 28.9 %copy-start.2 = (bf16[128,128]{1,0:T(8,128)(2,1)S(1)}, bf16[128,128]{1,0:T(8,128)(2,1)}, u32[]{:S(2)}) copy-start(bf16[128,128]{1,0:T(8,128)(2,1)} %refs_2_.1) | copy-start | bytes 98308
  2.1 28.9 %copy-start.4 = (s32[1,128]{1,0:T(1,128)S(1)}, s32[1,128]{1,0:T(1,128)}, u32[]{:S(2)}) copy-start(s32[1,128]{1,0:T(1,128)} %refs_6_.1) | copy-start | bytes 1540

commit v5 on v4

--- a/solution.py
+++ b/solution.py
@@ -46,6 +46,7 @@
     me = slot(z)
     for d in (2, nz - 2, 1, nz - 1):
         send(me, me, zs.at[d], zr.at[d], at_z(d))
+    yield 0
 
     def arrive(d, sem):
         block = slot((z + nz - d) % nz)
@@ -67,7 +68,34 @@
         yield d
 
 
-def gather_features(x_ref, vals_ref, out_ref, held_ref, zs, zr, ys, yr, loc, got):
+def order_slots(ids, count, cols, fast, groups):
+    slots = ids.shape[1]
+    down = lax.broadcasted_iota(jnp.int32, (slots, slots), 0)
+    along = lax.broadcasted_iota(jnp.int32, (slots, slots), 1)
+    ids = jnp.broadcast_to(ids.astype(F32), (slots, slots))
+    flip = jnp.sum(jnp.where(down == along, ids, 0.0), axis=1, keepdims=True)
+    p_down = jnp.floor(flip * (1.0 / cols))
+    q_down = jnp.where(down < count, jnp.broadcast_to(flip - p_down * cols, (slots, slots)), 1.0 * cols)
+    q_along = jnp.where(along < count, ids - jnp.floor(ids * (1.0 / cols)) * cols, 1.0 * cols)
+    same = jnp.where((q_along == q_down) & (along < down), 1.0, 0.0)
+    before = jnp.where(q_along < q_down, 1.0, 0.0) + same
+    rank = jnp.sum(before, axis=1, keepdims=True)
+    keep = jnp.minimum(jnp.sum(same, axis=1, keepdims=True), 1.0)
+    half = jnp.floor(p_down * (1.0 / fast))
+    source = (p_down - half * fast) * groups + half
+    here = jnp.where(rank == along.astype(F32), 1.0, 0.0)
+
+    def placed(value):
+        return jnp.sum(here * value, axis=0, keepdims=True).astype(jnp.int32)
+
+    column = along.astype(F32)
+    upto = jnp.sum(jnp.where(q_down <= column, 1.0, 0.0), axis=0, keepdims=True)
+    count_in = jnp.sum(jnp.where(q_down == column, 1.0, 0.0), axis=0, keepdims=True)
+    last = jnp.where(count_in > 0.0, upto - 1.0, 1.0 * slots).astype(jnp.int32)
+    return placed(down.astype(F32)), placed(source), placed(keep), last
+
+
+def gather_features(x_ref, ids_ref, count_ref, vals_ref, out_ref, held_ref, tab_ref, zs, zr, ys, yr, loc, got, *, groups):
     r, c = lax.axis_index("row"), lax.axis_index("col")
     nz = out_ref.shape[0] // YL
     z, y = r // YL, r % YL
@@ -91,7 +119,12 @@
 
     own.wait()
     send(out_ref.at[r], out_ref.at[r], ys.at[0], yr.at[0], side)
-    for d in spread_along_z(z, nz, turn, at_z, lambda at: out_ref.at[at * YL + y], zs, zr, send):
+    spread = spread_along_z(z, nz, turn, at_z, lambda at: out_ref.at[at * YL + y], zs, zr, send)
+    next(spread)
+    table = order_slots(ids_ref[...], count_ref[0, 0], nz * YL, C, groups)
+    for n in range(4):
+        tab_ref[n : n + 1, :] = table[n]
+    for d in spread:
         block = out_ref.at[(z + nz - d) % nz * YL + y]
         send(block, block, ys.at[d], yr.at[d], side)
     for d in range(nz):
@@ -102,20 +135,16 @@
     blocks.wait()
 
 
-def multiply(ids_ref, count_ref, vals_ref, src_ref, out_ref, tab_ref, last_ref, acc, spot, head):
-    count, cols, slots = count_ref[0, 0], src_ref.shape[0], ids_ref.shape[1]
+def multiply(ids_ref, count_ref, vals_ref, src_ref, out_ref, acc):
+    count, cols = count_ref[0, 0], src_ref.shape[0]
     dead = acc.shape[0] - 1
     acc[...] = jnp.zeros_like(acc)
-    for q in range(cols):
-        spot[q] = 0
-
     def step(j, _):
         for half in range(0, CHUNK, 4):
             made = []
             for i in range(4):
                 k = j * CHUNK + half + i
                 p, q = ids_ref[0, k] // cols, ids_ref[0, k] % cols
-                spot[q] = spot[q] + jnp.where(k < count, 1, 0)
                 got = jnp.dot(vals_ref[k], src_ref[q], preferred_element_type=F32)
                 made.append((jnp.where(k < count, p, dead), got))
             for to, got in made:
@@ -123,36 +152,12 @@
         return 0
 
     lax.fori_loop(0, (count + CHUNK - 1) // CHUNK, step, 0)
-    begin = jnp.int32(0)
-    for q in range(cols):
-        n = spot[q]
-        spot[q] = begin
-        head[q] = begin
-        begin = begin + n
-        last_ref[0, q] = jnp.where(n > 0, begin - 1, slots)
-
-    def place(k, _):
-        p, q = ids_ref[0, k] // cols, ids_ref[0, k] % cols
-        at = spot[q]
-        spot[q] = at + 1
-        tab_ref[0, at] = k
-        tab_ref[1, at] = p % C * (dead // C) + p // C
-        tab_ref[2, at] = jnp.where(at == head[q], 0, 1)
-        return 0
-
-    def blank(k, _):
-        for n in range(3):
-            tab_ref[n, k] = 0
-        return 0
-
-    lax.fori_loop(0, count, place, 0)
-    lax.fori_loop(count, slots, blank, 0)
     for b in range(dead):
         out_ref[b % C * (dead // C) + b // C] = acc[b].astype(BF16)
 
 
 def reduce_step_and_back(
-    part_ref, grad_ref, w_ref, tab_ref, last_ref, vals_ref, perm_ref, out_ref, wout_ref,
+    part_ref, grad_ref, w_ref, tab_ref, vals_ref, perm_ref, out_ref, wout_ref,
     part, sib, sx, rel, rx, sy, ry, share, wpart, wx, wy, grads, sums, back, zsib, sz, rz, wz, wall, loc,
     cs, cr, rs, rr, xs, xr, hs, hr, gys, gyr, gxs, gxr, gcs, gcr, wxs, wxr, wys, wyr,
     ys, yr, zs, zr, wzs, wzr, was, war,
@@ -330,13 +335,13 @@
     lax.fori_loop(0, (sums.shape[0] - 1) // CHUNK, step, jnp.zeros((BLOCK, HIDDEN), F32))
     for d in far_first(nz) + [0]:
         to = (z + d) % nz
-        back[to] = sums[last_ref[0, to * YL + 1 - y]].astype(BF16)
+        back[to] = sums[tab_ref[3, to * YL + 1 - y]].astype(BF16)
         send(back.at[to], zsib.at[to], ys.at[d], yr.at[d], side_y)
 
     def both(d):
         to = (z + d) % nz
         remote(back.at[to], zsib.at[to], ys.at[d], yr.at[d], side_y).wait_recv()
-        return sums[last_ref[0, to * YL + y]] + zsib[to].astype(F32)
+        return sums[tab_ref[3, to * YL + y]] + zsib[to].astype(F32)
 
     for d in far_first(nz):
         to = (z + d) % nz
@@ -381,35 +386,28 @@
     ids = block_ids[0]
     piece = BLOCK // C // X
 
-    source, vals = pl.pallas_call(
-        gather_features,
+    slots = block_ids.shape[-1]
+    source, vals, table = pl.pallas_call(
+        lambda *refs: gather_features(*refs, groups=cols // C),
         out_shape=(
             jax.ShapeDtypeStruct((rows,) + blk, BF16),
             jax.ShapeDtypeStruct(block_vals.shape[2:], BF16),
+            jax.ShapeDtypeStruct((4, slots), jnp.int32),
         ),
-        in_specs=[VMEM, pl.BlockSpec(memory_space=pltpu.HBM)],
-        out_specs=(VMEM, VMEM),
+        in_specs=[VMEM, VMEM, SMEM, pl.BlockSpec(memory_space=pltpu.HBM)],
+        out_specs=(VMEM, VMEM, VMEM),
         scratch_shapes=[dma(nz), dma(nz), dma(nz), dma(nz), dma(), dma()],
         compiler_params=pltpu.CompilerParams(collective_id=0, has_side_effects=True, vmem_limit_bytes=WIDE),
         cost_estimate=LONG,
         name="gather_features",
-    )(features, block_vals[0, 0])
-
-    slots = block_ids.shape[-1]
-    part, table, last = pl.pallas_call(
+    )(features, ids, block_count, block_vals[0, 0])
+
+    part = pl.pallas_call(
         multiply,
-        out_shape=(
-            jax.ShapeDtypeStruct((cols,) + blk, BF16),
-            jax.ShapeDtypeStruct((3, slots), jnp.int32),
-            jax.ShapeDtypeStruct((1, rows), jnp.int32),
-        ),
+        out_shape=jax.ShapeDtypeStruct((cols,) + blk, BF16),
         in_specs=[SMEM, SMEM, VMEM, VMEM],
-        out_specs=(VMEM, SMEM, SMEM),
-        scratch_shapes=[
-            pltpu.VMEM((cols + 1,) + blk, F32),
-            pltpu.SMEM((rows,), jnp.int32),
-            pltpu.SMEM((rows,), jnp.int32),
-        ],
+        out_specs=VMEM,
+        scratch_shapes=[pltpu.VMEM((cols + 1,) + blk, F32)],
         compiler_params=pltpu.CompilerParams(vmem_limit_bytes=LIMIT),
         name="aggregate",
     )(ids, block_count, vals, source)
@@ -417,7 +415,7 @@
     return pl.pallas_call(
         lambda *refs: reduce_step_and_back(*refs, scale=scale),
         out_shape=(jax.ShapeDtypeStruct(blk, BF16), jax.ShapeDtypeStruct((BLOCK, HIDDEN), F32)),
-        in_specs=[HBM, VMEM, VMEM, SMEM, SMEM, VMEM, VMEM],
+        in_specs=[HBM, VMEM, VMEM, SMEM, VMEM, VMEM],
         out_specs=(VMEM, VMEM),
         scratch_shapes=[
             pltpu.VMEM((X, YH) + blk, BF16),
@@ -450,7 +448,7 @@
         ),
         cost_estimate=LONG,
         name="reduce_step_and_back",
-    )(part.reshape((C, X, YH) + blk), grad_out, weight, table, last, vals, node_perm)
+    )(part.reshape((C, X, YH) + blk), grad_out, weight, table, vals, node_perm)
 
 
 def solution(mesh):

time: 85.7 us -> 83.7 us (0.977)
  Pallas kernels: 82 us -> 79.7 us
    pallas_call x2, Pallas kernels: 28.8 us -> 21.9 us  [the longest x1 20.2 us: shards(): pl.pallas_call(lambda *refs: gather_features(*refs, groups=cols // C), ou...]
    pallas_call x1, Pallas kernels: 53.2 us -> 57.8 us  [shards(): pl.pallas_call(lambda *refs: reduce_step_and_back(*refs, scale=scale), ou...]
where the time goes in v5:
time: 83.7 us; the launch traced here: 83.8 us
  Pallas kernels  79.7 us (95%)
  local copies, waits for them, and re-layouts  2.69 us (3%)
  between operations  1.34 us (2%)
    pallas_call x1, Pallas kernels, shards(): pl.pallas_call(lambda *refs: reduce_step_and_back(*refs, scale=scale), ou...  57.8 us
    pallas_call x1, Pallas kernels, shards(): pl.pallas_call(lambda *refs: gather_features(*refs, groups=cols // C), ou...  20.2 us
    unnamed x12, local copies, waits for them, and re-layouts  2.69 us
    pallas_call x1, Pallas kernels, shards(): pl.pallas_call(multiply, out_shape=jax.ShapeDtypeStruct((cols,) + blk, BF...  1.75 us

profile of v5, /device:TPU:1, one launch (start us, length us, event | category | flops | bytes accessed | tf_op | source)
XLA Modules:
  0.0 83.8 jit_solution(2316413640161053988)
XLA Ops:
  1.3 0.0 copy-start
  1.3 0.7 copy-done
  2.0 0.0 copy-start.3
  2.0 0.7 copy-done.3
  2.7 0.0 copy-start.1
  2.7 0.0 copy-start.2
  2.7 0.0 copy-start.4
  2.7 20.2 %gather_features.1 = (bf16[16,128,128]{2,1,0:T(8,128)(2,1)S(1)}, bf16[152,128,128]{2,1,0:T(8,128)(2,1)S(1)}, s32[4,152]{1,0:T(4,128)S(1)}) custom-call(bf16[128,128]{1,0:T(8,128)(2,1)S(1)} %copy-done, s32[1,152]{1,0:T(1,128)S(1)} %bitcast.4, s32[1,1]{1,0:T(1,128)S(6)} %copy.11.refs_2_.count_ref, bf16[152,128,128]{2,1,0:T(8,128)(2,1)} %bitcast.6), custom_call_target="tpu_custom_call" | custom-call | bytes 50000000 | tf_op jit(solution)/shard_map/gather_features/pallas_call | solution.py:390
  22.9 1.8 %aggregate.1 = bf16[32,128,128]{2,1,0:T(8,128)(2,1)S(1)} custom-call(s32[1,152]{1,0:T(1,128)S(1)} %bitcast.5, s32[1,1]{1,0:T(1,128)S(6)} %copy.11.refs_2_.count_ref, bf16[152,128,128]{2,1,0:T(8,128)(2,1)S(1)} %get-tuple-element.5.vals_ref.refs_4_, bf16[16,128,128]{2,1,0:T(8,128)(2,1)S(1)} %get-tuple-element.6.src_ref), custom_call_target="tpu_custom_call" | custom-call | tf_op jit(solution)/shard_map/aggregate/pallas_call | solution.py:405
  24.7 0.0 copy-done.1
  24.7 0.0 copy-done.2
  24.7 0.0 copy-done.4
  24.7 57.8 %reduce_step_and_back.1 = (bf16[128,128]{1,0:T(8,128)(2,1)S(1)}, f32[128,128]{1,0:T(8,128)S(1)}) custom-call(bf16[2,4,4,128,128]{4,3,2,1,0:T(8,128)(2,1)S(1)} %bitcast.3, bf16[128,128]{1,0:T(8,128)(2,1)S(1)} %copy-done.1, bf16[128,128]{1,0:T(8,128)(2,1)S(1)} %copy-done.2, s32[4,152]{1,0:T(4,128)S(1)} %get-tuple-element.7.refs_3_, ...), custom_call_target="tpu_custom_call" | custom-call | bytes 50000000 | tf_op jit(solution)/shard_map/reduce_step_and_back/pallas_call | solution.py:415
  82.5 0.6 copy.12
  83.1 0.6 copy.13
Async XLA Ops:
  1.3 0.8 copy-start
  2.0 0.7 copy-start.3
  2.7 22.0 %copy-start.1 = (bf16[128,128]{1,0:T(8,128)(2,1)S(1)}, bf16[128,128]{1,0:T(8,128)(2,1)}, u32[]{:S(2)}) copy-start(bf16[128,128]{1,0:T(8,128)(2,1)} %refs_1_.1) | copy-start | bytes 98308
  2.7 22.0 %copy-start.2 = (bf16[128,128]{1,0:T(8,128)(2,1)S(1)}, bf16[128,128]{1,0:T(8,128)(2,1)}, u32[]{:S(2)}) copy-start(bf16[128,128]{1,0:T(8,128)(2,1)} %refs_2_.2) | copy-start | bytes 98308
  2.7 22.0 %copy-start.4 = (s32[1,128]{1,0:T(1,128)S(1)}, s32[1,128]{1,0:T(1,128)}, u32[]{:S(2)}) copy-start(s32[1,128]{1,0:T(1,128)} %refs_5_.1) | copy-start | bytes 1540
